TPU v7x, 32 devices: a whole 2x2x4 slice. The times are simulated.
32 devices in a mesh: group: 1, expert: 16 (over z, y, x), step: 2 (over core).
Axes of the slice: x: 2, y: 2, z: 4, core: 2. Of those that a mesh axis runs over, the one named last changes fastest.
Arguments:
- latents: float32 [2, 2048, 1536], P('step', ('group', 'expert')), may hold values from -6 to 6
- modulation: float32 [2, 6, 1536], P('group'), may hold values from -3 to 3
- shallow_routes: int32 [2, 2048, 2], P('step', ('group', 'expert')), may hold values from 0 to 3, all different within a row; in each aligned block of 128 rows (0 to 127, 128 to 255, ..., all dimensions but the last counted through in order) at most 64 rows name the same one
- deep_routes: int32 [2048, 2], P(('group', 'expert')), may hold values from 0 to 3, all different within a row; in each aligned block of 128 rows (0 to 127, 128 to 255, ...) at most 64 rows name the same one
- refresh: int32 [16], P(('group', 'expert')), may hold values from 0 to 1
- shallow_in: bfloat16 [16, 1536, 768], P('expert'), may hold values from -0.15625 to 0.15625
- shallow_out: bfloat16 [16, 768, 1536], P('expert'), may hold values from -0.109375 to 0.109375
- deep_in: bfloat16 [16, 1536, 768], P('expert'), may hold values from -0.15625 to 0.15625
- deep_out: bfloat16 [16, 768, 1536], P('expert'), may hold values from -0.109375 to 0.109375
- shallow_router: float32 [1536, 4], replicated, may hold values from -0.15625 to 0.15625
- deep_router: float32 [1536, 4], replicated, may hold values from -0.15625 to 0.15625
Outputs:
- result: bfloat16 [2, 2048, 1536], P('step', ('group', 'expert'))
Inputs may be any that keep to these rules, and one draw needn't show every extreme that they name: `shallow_routes`: within the 128 rows of one index of expert (aligned blocks), each expert is named by at most 64 rows, and by exactly 64 rows in some block; a row names two different experts. `deep_routes`: within the 128 rows of one index of expert (aligned blocks), each expert is named by at most 64 rows, and by exactly 64 rows in some block; a row names two different experts.
All inputs are finite; a program needn't handle non-finite values.
Results may differ from a plain program's by a relative error of at most 0.01.
Values may be sent and summed in bfloat16 or wider, within the bound.
No kernel may reach another device: no remote copies, remote signals or barrier semaphores. Data moves between devices by JAX's collectives and lax.ppermute only.
A program may use at most 64 MiB of HBM per device.

v0:
```python
import jax
import jax.numpy as jnp
from jax import lax
from jax.sharding import PartitionSpec as P


def from_root(block, axis, owner):
    block = jnp.where(lax.axis_index(axis) == owner, block, jnp.zeros_like(block))
    return lax.psum(block, axis)


def modulate(hidden, shift_row, scale_row):
    average = jnp.mean(hidden, axis=-1, keepdims=True)
    centred = hidden - average
    variance = jnp.mean(centred * centred, axis=-1, keepdims=True)
    return (centred * lax.rsqrt(variance + 1e-06) * (1.0 + scale_row) + shift_row).astype(
        jnp.bfloat16
    )


def plan(normed, routes, router, capacity):
    rows_count, width = normed.shape
    experts = router.shape[1]
    logits = jnp.dot(normed.astype(jnp.float32), router, precision=lax.Precision.HIGHEST)
    hits = routes[:, :, None] == jnp.arange(experts, dtype=jnp.int32)
    chosen = jnp.sum(jnp.where(hits, logits[:, None, :], 0.0), axis=-1)
    gate_sig = jax.nn.sigmoid(chosen)
    weights = gate_sig / jnp.sum(gate_sig, axis=-1, keepdims=True)
    pair_hits = hits.reshape(rows_count * 2, experts).astype(jnp.int32)
    position = jnp.sum(pair_hits * (jnp.cumsum(pair_hits, axis=0) - 1), axis=-1).reshape(
        rows_count, 2
    )
    slot_hit = position[:, :, None] == jnp.arange(capacity, dtype=jnp.int32)
    placed = hits[:, :, :, None] & slot_hit[:, :, None, :]
    dispatch = jnp.any(placed, axis=1).reshape(rows_count, experts * capacity).astype(jnp.bfloat16)
    gathered = jnp.einsum("rs,rd->sd", dispatch, normed, preferred_element_type=jnp.float32).astype(
        jnp.bfloat16
    )
    combine_w = jnp.sum(jnp.where(placed, weights[:, :, None, None], 0.0), axis=1)
    return (gathered.reshape(experts, capacity, width), combine_w)


def spread(gathered, slices):
    experts, capacity, width = gathered.shape
    quarters = slices // experts
    return jnp.broadcast_to(gathered[:, None], (experts, quarters, capacity, width)).reshape(
        slices, capacity, width
    )


def expert_rows(piece, weight_in, weight_out):
    dims = piece.shape
    flat_rows = piece.reshape(-1, dims[-1])
    hidden = jax.nn.gelu(
        jnp.dot(flat_rows, weight_in, preferred_element_type=jnp.float32), approximate=True
    ).astype(jnp.bfloat16)
    return (
        jnp.dot(hidden, weight_out, preferred_element_type=jnp.float32)
        .astype(jnp.bfloat16)
        .reshape(dims)
    )


def combine(summed, combine_w):
    rows_count = combine_w.shape[0]
    width = summed.shape[-1]
    return jnp.dot(
        combine_w.reshape(rows_count, -1),
        summed.reshape(-1, width),
        precision=lax.Precision.HIGHEST,
        preferred_element_type=jnp.float32,
    )


def finish(returned, combine_w):
    experts = combine_w.shape[1]
    width = returned.shape[2]
    summed = jnp.sum(
        returned.astype(jnp.float32).reshape(experts, -1, returned.shape[1], width), axis=1
    )
    return combine(summed, combine_w)


def body(
    latents,
    modulation,
    shallow_routes,
    deep_routes,
    refresh,
    shallow_in,
    shallow_out,
    deep_in,
    deep_out,
    shallow_router,
    deep_router,
):
    slices = lax.axis_size("expert")
    experts = shallow_router.shape[1]
    rows_count = latents.shape[1]
    capacity = 2 * max(rows_count * 5 // 64, rows_count // experts)
    step_idx = lax.axis_index("step")
    root_idx = refresh[0]
    own_mod = lax.dynamic_index_in_dim(modulation, step_idx, 0, keepdims=False)
    features = latents[0]
    normed = modulate(features, own_mod[0], own_mod[1])
    gathered, combine_w = plan(normed, shallow_routes[0], shallow_router, capacity)
    partial_value = expert_rows(
        lax.all_to_all(spread(gathered, slices), "expert", split_axis=0, concat_axis=0, tiled=True),
        shallow_in[0],
        shallow_out[0],
    )
    returned = lax.all_to_all(partial_value, "expert", split_axis=0, concat_axis=0, tiled=True)
    moe_shallow = finish(returned, combine_w)
    after_shallow = (features + own_mod[2] * moe_shallow).astype(jnp.bfloat16)
    normed_deep = modulate(after_shallow.astype(jnp.float32), own_mod[3], own_mod[4])
    gathered_deep, combine_deep = plan(normed_deep, deep_routes, deep_router, capacity)
    partial_value = expert_rows(
        lax.all_to_all(
            spread(gathered_deep, slices), "expert", split_axis=0, concat_axis=0, tiled=True
        ),
        deep_in[0],
        deep_out[0],
    )
    returned_deep = lax.all_to_all(partial_value, "expert", split_axis=0, concat_axis=0, tiled=True)
    moe_deep = finish(returned_deep, combine_deep)
    own_delta = (own_mod[5] * moe_deep).astype(jnp.bfloat16)
    deep_delta = from_root(own_delta, "step", root_idx)
    result = (after_shallow.astype(jnp.float32) + deep_delta.astype(jnp.float32)).astype(
        jnp.bfloat16
    )
    return result[None]


def solution(mesh):
    in_specs = (
        P("step", ("group", "expert"), None),
        P("group", None, None),
        P("step", ("group", "expert"), None),
        P(("group", "expert"), None),
        P(("group", "expert")),
        P("expert", None, None),
        P("expert", None, None),
        P("expert", None, None),
        P("expert", None, None),
        P(),
        P(),
    )
    out_specs = P("step", ("group", "expert"), None)
    return jax.shard_map(body, mesh=mesh, in_specs=in_specs, out_specs=out_specs, check_vma=False)
```

profile of v0, /device:TPU:0, one launch (start us, length us, event | category | flops | bytes accessed | tf_op | source)
XLA Modules:
  0.0 376.2 jit_solution(6678324923360058093)
XLA Ops:
  6.5 0.9 copy.32
  7.5 0.1 eq.123
  7.6 0.1 eq.119
  7.8 1.3 reduce_sum.127
  9.0 1.4 multiply_reduce_fusion.1
  10.4 0.7 iota_compare_fusion.5
  11.1 1.2 reduce-window.14
  12.3 0.1 slice.46
  12.4 0.1 copy.34
  12.5 0.1 copy.35
  12.6 0.1 add_bitcast_fusion.1
  12.7 0.1 eq.127
  12.9 0.1 copy.36
  13.0 0.9 dynamic-slice_reduce_fusion.1
  13.9 1.6 convolution_convert_fusion.3
  15.6 0.3 broadcast_in_dim.82
  15.9 79.5 %all_to_all.20 = bf16[16,64,1536]{2,1,0:T(8,128)(2,1)} all-to-all(bf16[16,64,1536]{2,1,0:T(8,128)(2,1)S(1)} %bitcast.112), channel_id=1, replica_groups=mesh['group'=1,'expert'=16,'step'=2] {'expert'}, dimensions={0} | all-to-all | bytes 6291456 | tf_op jit(solution)/shard_map/all_to_all | solution.py:108
  95.4 10.4 %convolution_convert_fusion.1 = bf16[1024,1536]{1,0:T(8,128)(2,1)} fusion(bf16[1,768,1536]{2,1,0:T(8,128)(2,1)S(1)} %copy-done, bf16[1024,1536]{1,0:T(8,128)(2,1)} %bitcast.116, bf16[1,1536,768]{2,1,0:T(8,128)(2,1)} %param.16), kind=kOutput, calls=%fused_computation.5 | convolution fusion | flops 4840488960 | bytes 11010048 | tf_op jit(solution)/shard_map/dot_general | solution.py:58
  105.8 4.6 %all-to-all-start.1 = ((bf16[16,64,1536]{2,1,0:T(8,128)(2,1)}), bf16[16,64,1536]{2,1,0:T(8,128)(2,1)}, u32[]{:S(2)}, u32[]{:S(2)}) async-start(bf16[16,64,1536]{2,1,0:T(8,128)(2,1)} %bitcast.114), calls=%async_computation.1 | async-start | bytes 6291456 | tf_op jit(solution)/shard_map/all_to_all | solution.py:112
  110.5 0.1 copy.37
  110.6 0.1 eq.139
  110.7 0.1 eq.135
  110.9 1.2 reduce-window.16
  112.1 0.1 slice.47
  112.2 0.1 copy.39
  112.3 0.1 copy.40
  112.4 0.1 add_bitcast_fusion
  112.5 0.1 eq.143
  112.7 0.1 copy.41
  112.7 0.5 fusion.44
  113.5 57.2 %all-to-all-done.1 = bf16[16,64,1536]{2,1,0:T(8,128)(2,1)} async-done(((bf16[16,64,1536]{2,1,0:T(8,128)(2,1)}), bf16[16,64,1536]{2,1,0:T(8,128)(2,1)}, u32[]{:S(2)}, u32[]{:S(2)}) %all-to-all-start.1) | async-done | bytes 3145760 | tf_op jit(solution)/shard_map/all_to_all | solution.py:112
  170.7 2.6 convert_reduce_fusion.1
  173.2 1.1 fusion.61
  174.3 0.2 multiply_reduce_fusion
  174.6 0.2 add_convert_fusion.1
  174.8 0.3 convolution_convert_fusion.2
  175.1 0.1 copy-done.2
  175.2 0.3 broadcast_in_dim.86
  175.5 84.7 %all_to_all.21 = bf16[16,64,1536]{2,1,0:T(8,128)(2,1)} all-to-all(bf16[16,64,1536]{2,1,0:T(8,128)(2,1)S(1)} %bitcast.113), channel_id=1, replica_groups=mesh['group'=1,'expert'=16,'step'=2] {'expert'}, dimensions={0} | all-to-all | bytes 6291456 | tf_op jit(solution)/shard_map/all_to_all | solution.py:118
  260.3 11.1 %convolution_convert_fusion = bf16[1024,1536]{1,0:T(8,128)(2,1)} fusion(bf16[1,768,1536]{2,1,0:T(8,128)(2,1)} %param.19, bf16[1024,1536]{1,0:T(8,128)(2,1)} %bitcast.117, bf16[1,1536,768]{2,1,0:T(8,128)(2,1)} %param.18), kind=kOutput, calls=%fused_computation.4 | convolution fusion | flops 4840488960 | bytes 11010048 | tf_op jit(solution)/shard_map/dot_general | solution.py:58
  271.4 4.6 %all-to-all-start.3 = ((bf16[16,64,1536]{2,1,0:T(8,128)(2,1)}), bf16[16,64,1536]{2,1,0:T(8,128)(2,1)}, u32[]{:S(2)}, u32[]{:S(2)}) async-start(bf16[16,64,1536]{2,1,0:T(8,128)(2,1)} %bitcast.115), calls=%async_computation.3 | async-start | bytes 6291456 | tf_op jit(solution)/shard_map/all_to_all | solution.py:124
  276.7 0.4 fusion.62
  277.2 0.1 fusion.46
  277.3 58.9 %all-to-all-done.3 = bf16[16,64,1536]{2,1,0:T(8,128)(2,1)} async-done(((bf16[16,64,1536]{2,1,0:T(8,128)(2,1)}), bf16[16,64,1536]{2,1,0:T(8,128)(2,1)}, u32[]{:S(2)}, u32[]{:S(2)}) %all-to-all-start.3) | async-done | bytes 3145760 | tf_op jit(solution)/shard_map/all_to_all | solution.py:124
  336.2 2.6 convert_reduce_fusion
  338.7 1.7 fusion.22
  340.5 27.0 %all-reduce.2.cloned.1.call-done = bf16[128,1536]{1,0:T(8,128)(2,1)} async-done(((bf16[128,1536]{1,0:T(8,128)(2,1)}), bf16[128,1536]{1,0:T(8,128)(2,1)}) %all-reduce.2.cloned.1.call-update) | async-done | bytes 393232 | tf_op jit(solution)/shard_map/psum | solution.py:9
  367.6 1.8 fusion.39
  (41 shorter events, 0.5 us)
Async XLA Ops:
  6.5 88.8 %copy-start = (bf16[1,768,1536]{2,1,0:T(8,128)(2,1)S(1)}, bf16[1,768,1536]{2,1,0:T(8,128)(2,1)}, u32[]{:S(2)}) copy-start(bf16[1,768,1536]{2,1,0:T(8,128)(2,1)} %param.17) | copy-start | bytes 7077892
  105.8 4.7 %copy-start.7 = (s32[128,2]{0,1:T(2,128)S(1)}, s32[128,2]{0,1:T(2,128)}, u32[]{:S(2)}) copy-start(s32[128,2]{0,1:T(2,128)} %param.14) | copy-start | bytes 3076
  105.8 6.9 %copy-start.1 = (f32[1,128,1536]{2,1,0:T(8,128)S(1)}, f32[1,128,1536]{2,1,0:T(8,128)}, u32[]{:S(2)}) copy-start(f32[1,128,1536]{2,1,0:T(8,128)} %param.11) | copy-start | bytes 2359300
  105.8 6.9 %copy-start.4 = (f32[1536,4]{0,1:T(4,128)S(1)}, f32[1536,4]{0,1:T(4,128)}, u32[]{:S(2)}) copy-start(f32[1536,4]{0,1:T(4,128)} %param.20) | copy-start | bytes 73732
  105.8 7.4 %copy-start.6 = (s32[1,128,2]{1,2,0:T(2,128)S(1)}, s32[1,128,2]{1,2,0:T(2,128)}, u32[]{:S(2)}) copy-start(s32[1,128,2]{1,2,0:T(2,128)} %param.13) | copy-start | bytes 3076
  105.8 64.8 %all-to-all-start.1 = ((bf16[16,64,1536]{2,1,0:T(8,128)(2,1)}), bf16[16,64,1536]{2,1,0:T(8,128)(2,1)}, u32[]{:S(2)}, u32[]{:S(2)}) async-start(bf16[16,64,1536]{2,1,0:T(8,128)(2,1)} %bitcast.114), calls=%async_computation.1 | async-start | bytes 6291456 | tf_op jit(solution)/shard_map/all_to_all | solution.py:112
  174.3 0.9 copy-start.2
  271.4 5.3 %copy-start.5 = (f32[1536,4]{0,1:T(4,128)S(1)}, f32[1536,4]{0,1:T(4,128)}, u32[]{:S(2)}) copy-start(f32[1536,4]{0,1:T(4,128)} %param.21) | copy-start | bytes 73732
  271.4 64.8 %all-to-all-start.3 = ((bf16[16,64,1536]{2,1,0:T(8,128)(2,1)}), bf16[16,64,1536]{2,1,0:T(8,128)(2,1)}, u32[]{:S(2)}, u32[]{:S(2)}) async-start(bf16[16,64,1536]{2,1,0:T(8,128)(2,1)} %bitcast.115), calls=%async_computation.3 | async-start | bytes 6291456 | tf_op jit(solution)/shard_map/all_to_all | solution.py:124
  276.0 91.6 %all-reduce.2.cloned.1.call-start = ((), (), s32[]{:S(2)}) async-start(), calls=%async_computation.4 | async-start | bytes 786432 | tf_op jit(solution)/shard_map/psum | solution.py:9
  277.3 90.3 %copy-start.3 = (f32[128,1536]{1,0:T(8,128)S(1)}, f32[128,1536]{1,0:T(8,128)}, u32[]{:S(2)}) copy-start(f32[128,1536]{1,0:T(8,128)} %copy-done.2) | copy-start | bytes 2359300
Sparse Core Ops, SparseCore 0:
  340.6 26.8 all-reduce.1
where the time goes:
time: 377 us; the launch traced here: 376 us
  blocking collectives  164 us (44%)
  waiting for transfers between devices  143 us (38%)
  matrix products  27.3 us (7%)
  other arithmetic  14.7 us (4%)
  between operations  14.3 us (4%)
  starting transfers between devices  9.3 us (2%)
    all_to_all x2, waiting for transfers between devices, body(): lax.all_to_all(partial_value, 'expert', split_axis=0, concat_axis=0, tile...  116 us
    all_to_all x1, blocking collectives, body(): lax.all_to_all(spread(gathered_deep, slices), 'expert', split_axis=0, con...  84.7 us
    all_to_all x1, blocking collectives, body(): lax.all_to_all(spread(gathered, slices), 'expert', split_axis=0, concat_a...  79.5 us
    psum x1, waiting for transfers between devices, from_root(): return lax.psum(block, axis)  27 us
    dot_general x2, matrix products, expert_rows(): jnp.dot(hidden, weight_out, preferred_element_type=jnp.float32)  21.5 us
    all_to_all x2, starting transfers between devices, body(): lax.all_to_all(partial_value, 'expert', split_axis=0, concat_axis=0, tile...  9.25 us
  transfers between devices with their start and end apart: 3, of which 3 were waited for; matrix products, arithmetic and copies ran while one was open for 1% of the time, Pallas kernels for 0%

commit v1 on v0

v1 whole, which is shorter than its diff:
```python
import functools

import jax
import jax.numpy as jnp
from jax import lax
from jax.experimental import pallas as pl
from jax.experimental.pallas import tpu as pltpu
from jax.sharding import PartitionSpec as P

BF = jnp.bfloat16
F32 = jnp.float32
VMEM = pltpu.VMEM
SMEM = pltpu.SMEM


def pieces3(value):
    high = value.astype(BF)
    rest = value - high.astype(F32)
    middle = rest.astype(BF)
    low = (rest - middle.astype(F32)).astype(BF)
    return high, middle, low


def normalise(hidden, shift_row, scale_row):
    average = jnp.mean(hidden, axis=-1, keepdims=True)
    centred = hidden - average
    variance = jnp.mean(centred * centred, axis=-1, keepdims=True)
    return (centred * lax.rsqrt(variance + 1e-06) * (1.0 + scale_row) + shift_row).astype(BF)


def slot_rows(routes, weights, home, core, experts, half):
    padded = max(8, experts)
    tokens = routes.shape[1]
    relative = routes ^ home
    number = lax.broadcasted_iota(jnp.int32, (padded, tokens), 0)
    first, second = number == relative[0:1], number == relative[1:2]
    hits = first | second
    before = lax.broadcasted_iota(jnp.int32, (tokens, tokens), 0) < lax.broadcasted_iota(
        jnp.int32, (tokens, tokens), 1
    )
    ones = jnp.where(hits, 1.0, 0.0).astype(BF)
    place = jnp.dot(ones, jnp.where(before, 1.0, 0.0).astype(BF), preferred_element_type=F32)
    columns = [jnp.where(hits, place, -1.0).astype(BF)]
    if weights is not None:
        per_expert = jnp.where(first, weights[0:1], jnp.where(second, weights[1:2], 0.0))
        columns.extend(pieces3(per_expert))
    table = jnp.concatenate(columns, axis=1)
    rows = 2 * experts * half
    slot = lax.broadcasted_iota(jnp.int32, (rows, padded), 0)
    block = jnp.where(slot >= experts * half, slot - experts * half, slot)
    owner = lax.broadcasted_iota(jnp.int32, (rows, padded), 1)
    spread = (block >= owner * half) & (block < (owner + 1) * half)
    wide = jnp.dot(jnp.where(spread, 1.0, 0.0).astype(BF), table, preferred_element_type=F32)
    slot = lax.broadcasted_iota(jnp.int32, (rows, tokens), 0)
    other = slot >= experts * half
    block = jnp.where(other, slot - experts * half, slot)
    within = block
    for step in range(1, experts):
        within = within - jnp.where(block >= step * half, half, 0)
    within = within + jnp.where(other, (1 - core) * half, core * half)
    taken = wide[:, :tokens] == within.astype(F32)
    if weights is None:
        return jnp.where(taken, 1.0, 0.0).astype(BF)
    parts = [
        jnp.where(taken, wide[:, (k + 1) * tokens : (k + 2) * tokens], 0.0).astype(BF)
        for k in range(3)
    ]
    return jnp.concatenate(parts, axis=1)


def gate_pack(normed, routes, router_t, experts):
    tokens = normed.shape[0]
    stacked = jnp.concatenate(pieces3(router_t), axis=0)
    logits3 = lax.dot_general(
        stacked, normed, (((1,), (1,)), ((), ())), preferred_element_type=F32
    )
    count = router_t.shape[0]
    logits = logits3[:count] + logits3[count : 2 * count] + logits3[2 * count :]
    number = lax.broadcasted_iota(jnp.int32, (count, tokens), 0)
    gates = []
    for k in range(2):
        chosen = jnp.sum(jnp.where(number == routes[k : k + 1], logits, 0.0), axis=0, keepdims=True)
        gates.append(jax.nn.sigmoid(chosen))
    total = gates[0] + gates[1]
    rows = [gates[0] / total, gates[1] / total, routes.astype(F32), jnp.zeros((4, tokens), F32)]
    return jnp.concatenate(rows, axis=0)


def mixed(rows_ref, pack, home, core, experts, half):
    tokens = pack.shape[1]
    routes = pack[2:4].astype(jnp.int32)
    weighted = slot_rows(routes, pack[0:2], home, core, experts, half)
    out3 = lax.dot_general(
        weighted, rows_ref[...], (((0,), (0,)), ((), ())), preferred_element_type=F32
    )
    return out3[:tokens] + out3[tokens : 2 * tokens] + out3[2 * tokens :]


def padded_router(ref, experts):
    value = ref[...]
    if experts < 8:
        value = jnp.concatenate([value, jnp.zeros((8 - experts, value.shape[1]), F32)], axis=0)
    return value


def pre_kernel(experts, half, scal, feats, mod, routes, router_t, keep, send, pack):
    home, core = scal[0], scal[1]
    normed = normalise(feats[...], mod[core, 0:1, :], mod[core, 1:2, :])
    onehot = slot_rows(routes[...], None, home, core, experts, half)
    rows = jnp.dot(onehot, normed, preferred_element_type=F32).astype(BF)
    keep[...] = rows[: experts * half]
    send[...] = rows[experts * half :]
    pack[...] = gate_pack(normed, routes[...], padded_router(router_t, experts), experts)


def gather_blocks(scratch, blocks):
    start = 0
    for block in blocks:
        scratch[start : start + block.shape[0], :] = block[...]
        start += block.shape[0]


def mid_kernel(experts, half, n_blocks, scal, *refs):
    blocks, refs = refs[:n_blocks], refs[n_blocks:]
    feats, feats_o, pack, pack_o, mod, routes, router_t, after, keep, pack_out, scratch = refs
    home, core, root = scal[0], scal[1], scal[2]
    is_root = core == root
    gather_blocks(scratch, blocks)
    moe = mixed(scratch, jnp.where(is_root, pack[...], pack_o[...]), home, core, experts, half)
    features = jnp.where(is_root, feats[...], feats_o[...])
    shallow = (features + mod[root, 2:3, :] * moe).astype(BF)
    after[...] = shallow
    normed = normalise(shallow.astype(F32), mod[root, 3:4, :], mod[root, 4:5, :])
    onehot = slot_rows(routes[...], None, home, core, experts, half)[: experts * half]
    keep[...] = jnp.dot(onehot, normed, preferred_element_type=F32).astype(BF)
    pack_out[...] = gate_pack(normed, routes[...], padded_router(router_t, experts), experts)


def rest_kernel(experts, half, n_blocks, scal, *refs):
    blocks, refs = refs[:n_blocks], refs[n_blocks:]
    feats, feats_o, pack, pack_o, mod, after, scratch = refs
    home, core, root = scal[0], scal[1], scal[2]
    is_root = core == root
    gather_blocks(scratch, blocks)
    moe = mixed(scratch, jnp.where(is_root, pack_o[...], pack[...]), home, core, experts, half)
    features = jnp.where(is_root, feats_o[...], feats[...])
    after[...] = (features + mod[1 - root, 2:3, :] * moe).astype(BF)


def last_kernel(experts, half, n_blocks, scal, *refs):
    blocks, refs = refs[:n_blocks], refs[n_blocks:]
    pack, mod, after_root, after_rest, result, scratch = refs
    home, core, root = scal[0], scal[1], scal[2]
    gather_blocks(scratch, blocks)
    moe = mixed(scratch, pack[...], home, core, experts, half)
    delta = (mod[root, 5:6, :] * moe).astype(BF)
    mine = jnp.where(core == root, after_root[...].astype(F32), after_rest[...].astype(F32))
    result[...] = (mine + delta.astype(F32)).astype(BF)


def expert_kernel(n_blocks, *refs):
    blocks, (w_in, w_out) = refs[:n_blocks], refs[n_blocks : n_blocks + 2]
    outs, scratch = refs[n_blocks + 2 : -1], refs[-1]
    gather_blocks(scratch, blocks)
    hidden = jnp.dot(scratch[...], w_in[...], preferred_element_type=F32)
    hidden = jax.nn.gelu(hidden, approximate=True).astype(BF)
    value = jnp.dot(hidden, w_out[...], preferred_element_type=F32).astype(BF)
    start = 0
    for out in outs:
        out[...] = value[start : start + out.shape[0]]
        start += out.shape[0]


def call(kernel, outs, scratch, args, flops, name):
    specs = [
        pl.BlockSpec(memory_space=SMEM if a.ndim == 1 else VMEM) for a in args
    ]
    nbytes = sum(a.size * a.dtype.itemsize for a in args) + sum(
        o.size * o.dtype.itemsize for o in outs
    )
    return pl.pallas_call(
        kernel,
        out_shape=outs,
        in_specs=specs,
        out_specs=[pl.BlockSpec(memory_space=VMEM)] * len(outs),
        scratch_shapes=scratch,
        compiler_params=pltpu.CompilerParams(vmem_limit_bytes=28 << 20),
        cost_estimate=pl.CostEstimate(flops=flops, bytes_accessed=nbytes, transcendentals=0),
        name=name,
    )(*args)


def struct(shape, dtype):
    return jax.ShapeDtypeStruct(shape, dtype)


class Links:
    def __init__(self, experts, quarters):
        self.experts, self.quarters = experts, quarters

    def plane(self, value, turn):
        quarters = self.quarters
        pairs = [
            (e * quarters + q, e * quarters + (q ^ turn))
            for e in range(self.experts)
            for q in range(quarters)
        ]
        return lax.ppermute(value, "expert", pairs)

    def far(self, value, turn):
        quarters = self.quarters
        pairs = [
            (e * quarters + q, (e ^ turn) * quarters + q)
            for e in range(self.experts)
            for q in range(quarters)
        ]
        return lax.ppermute(value, "expert", pairs)


def swap(value):
    return lax.ppermute(value, "step", [(0, 1), (1, 0)])


def expert_call(blocks, w_in, w_out):
    rows = sum(b.shape[0] for b in blocks)
    width, hidden = w_in.shape
    outs = [struct(b.shape, BF) for b in blocks]
    return call(
        functools.partial(expert_kernel, len(blocks)),
        outs,
        [pltpu.VMEM((rows, width), BF)],
        (*blocks, w_in, w_out),
        4 * rows * width * hidden,
        "expert_rows",
    )


def layer_half(rows, half, w_in, w_out, links, groups):
    experts = links.experts
    arrived = {}
    for turn in range(experts):
        block = rows[turn * half : (turn + 1) * half]
        arrived[turn] = links.far(block, turn) if turn else block
    back = {}
    for group in groups:
        mine = jnp.concatenate([arrived[t] for t in group], axis=0)
        cut = mine.shape[0] // 2
        from_x = links.plane(mine, 1)
        from_y = links.plane(mine, 2)
        diag_a = links.plane(from_x[:cut], 2)
        diag_b = links.plane(from_y[cut:], 1)
        own, px, py, pa, pb = expert_call([mine, from_x, from_y, diag_a, diag_b], w_in, w_out)
        via_y = links.plane(pa, 2)
        via_x = links.plane(pb, 1)
        to_x = jnp.concatenate(
            [(px[:cut].astype(F32) + via_y.astype(F32)).astype(BF), px[cut:]], axis=0
        )
        to_y = jnp.concatenate(
            [py[:cut], (py[cut:].astype(F32) + via_x.astype(F32)).astype(BF)], axis=0
        )
        total = (
            own.astype(F32)
            + links.plane(to_x, 1).astype(F32)
            + links.plane(to_y, 2).astype(F32)
        ).astype(BF)
        for k, turn in enumerate(group):
            block = total[k * half : (k + 1) * half]
            back[turn] = links.far(block, turn) if turn else block
    return [back[t] for t in range(experts)]


def both_cores(blocks, groups):
    other = {}
    for group in groups:
        joined = swap(jnp.concatenate([blocks[t] for t in group], axis=0))
        size = joined.shape[0] // len(group)
        for k, t in enumerate(group):
            other[t] = joined[k * size : (k + 1) * size]
    return blocks + [other[t] for t in range(len(blocks))]


def body(
    latents,
    modulation,
    shallow_routes,
    deep_routes,
    refresh,
    shallow_in,
    shallow_out,
    deep_in,
    deep_out,
    shallow_router,
    deep_router,
):
    slices = lax.axis_size("expert")
    experts = shallow_router.shape[1]
    quarters = slices // experts
    tokens, width = latents.shape[1:]
    half = max(tokens * 5 // 64, tokens // experts)
    links = Links(experts, quarters)
    core = lax.axis_index("step")
    home = lax.axis_index("expert") // quarters
    root = refresh[0]
    scal = jnp.stack([home, core, root]).astype(jnp.int32)
    is_root = core == root
    slots = experts * half
    partial = functools.partial
    cut = experts // 2
    groups = [list(range(cut)), list(range(cut, experts))]

    feats = latents[0]
    keep, send, pack = call(
        partial(pre_kernel, experts, half),
        [struct((slots, width), BF), struct((slots, width), BF), struct((8, tokens), F32)],
        [],
        (scal, feats, modulation, shallow_routes[0].T, shallow_router.T),
        4 * slots * tokens * width,
        "shallow_start",
    )
    got = swap(send)
    rows_root = jnp.where(is_root, keep, got)
    rows_rest = jnp.where(is_root, got, keep)
    pack_o = swap(pack)
    feats_o = swap(feats)
    scratch = [pltpu.VMEM((2 * slots, width), BF)]
    mix_flops = 12 * slots * tokens * width

    back_root = layer_half(rows_root, half, shallow_in[0], shallow_out[0], links, groups)
    blocks = both_cores(back_root, groups)
    after_root, rows_deep, pack_deep = call(
        partial(mid_kernel, experts, half, len(blocks)),
        [struct((tokens, width), BF), struct((slots, width), BF), struct((8, tokens), F32)],
        scratch,
        (scal, *blocks, feats, feats_o, pack, pack_o, modulation, deep_routes.T, deep_router.T),
        mix_flops,
        "shallow_end",
    )
    back_rest = layer_half(rows_rest, half, shallow_in[0], shallow_out[0], links, groups)
    blocks = both_cores(back_rest, groups)
    (after_rest,) = call(
        partial(rest_kernel, experts, half, len(blocks)),
        [struct((tokens, width), BF)],
        scratch,
        (scal, *blocks, feats, feats_o, pack, pack_o, modulation),
        mix_flops,
        "rest_end",
    )
    back_deep = layer_half(rows_deep, half, deep_in[0], deep_out[0], links, groups)
    blocks = both_cores(back_deep, groups)
    (result,) = call(
        partial(last_kernel, experts, half, len(blocks)),
        [struct((tokens, width), BF)],
        scratch,
        (scal, *blocks, pack_deep, modulation, after_root, after_rest),
        mix_flops,
        "deep_end",
    )
    return result[None]


def solution(mesh):
    in_specs = (
        P("step", ("group", "expert"), None),
        P("group", None, None),
        P("step", ("group", "expert"), None),
        P(("group", "expert"), None),
        P(("group", "expert")),
        P("expert", None, None),
        P("expert", None, None),
        P("expert", None, None),
        P("expert", None, None),
        P(),
        P(),
    )
    out_specs = P("step", ("group", "expert"), None)
    return jax.shard_map(body, mesh=mesh, in_specs=in_specs, out_specs=out_specs, check_vma=False)
```

time: 377 us -> 171 us (0.45)
  blocking collectives: 164 us -> 0 us
  waiting for transfers between devices: 143 us -> 65.4 us
  starting transfers between devices: 9.3 us -> 81.6 us
  matrix products: 27.3 us -> 0 us
  Pallas kernels: 0 us -> 17.5 us
  other arithmetic: 14.7 us -> 1.21 us
  between operations: 14.3 us -> 1.41 us
    all_to_all x2 -> x0, blocking collectives: 164 us -> none  [the longest x1 84.7 us: body(): lax.all_to_all(spread(gathered_deep, slices), 'expert', split_axis=0, con...]
    all_to_all x2 -> x0, waiting for transfers between devices: 116 us -> none  [body(): lax.all_to_all(partial_value, 'expert', split_axis=0, concat_axis=0, tile...]
    ppermute x0 -> x75, starting transfers between devices: none -> 81.6 us  [the longest x48 52.5 us: plane(): return lax.ppermute(value, 'expert', pairs)]
    ppermute x0 -> x75, waiting for transfers between devices: none -> 65.4 us  [the longest x48 33.2 us: plane(): return lax.ppermute(value, 'expert', pairs)]
    dot_general x8 -> x0, matrix products: 27.3 us -> none  [the longest x2 21.5 us: expert_rows(): jnp.dot(hidden, weight_out, preferred_element_type=jnp.float32)]
    psum x1 -> x0, waiting for transfers between devices: 27 us -> none  [from_root(): return lax.psum(block, axis)]
    pallas_call x0 -> x10, Pallas kernels: none -> 17.5 us  [call(): pl.pallas_call(kernel, out_shape=outs, in_specs=specs, out_specs=[pl.Bloc...]
    all_to_all x2 -> x0, starting transfers between devices: 9.25 us -> none  [body(): lax.all_to_all(partial_value, 'expert', split_axis=0, concat_axis=0, tile...]
  transfers between devices with their start and end apart: 3 -> 75, of which waited for: 3 -> 45; matrix products, arithmetic and copies ran while one was open for 1% -> 1% of each run, Pallas kernels for 0% -> 8%
where the time goes in v1:
time: 171 us
  starting transfers between devices  81.6 us (48%)
  waiting for transfers between devices  65.4 us (38%)
  Pallas kernels  17.5 us (10%)
  local copies, waits for them, and re-layouts  3.98 us (2%)
    ppermute x48, starting transfers between devices, plane(): return lax.ppermute(value, 'expert', pairs)  52.5 us
    ppermute x48, waiting for transfers between devices, plane(): return lax.ppermute(value, 'expert', pairs)  33.2 us
    ppermute x18, starting transfers between devices, far(): return lax.ppermute(value, 'expert', pairs)  28.2 us
    ppermute x18, waiting for transfers between devices, far(): return lax.ppermute(value, 'expert', pairs)  26.8 us
    pallas_call x10, Pallas kernels, call(): pl.pallas_call(kernel, out_shape=outs, in_specs=specs, out_specs=[pl.Bloc...  17.5 us
    ppermute x9, waiting for transfers between devices, swap(): return lax.ppermute(value, 'step', [(0, 1), (1, 0)])  5.46 us
    unnamed x24, local copies, waits for them, and re-layouts  3.51 us
  transfers between devices with their start and end apart: 75, of which 45 were waited for; matrix products, arithmetic and copies ran while one was open for 1% of the time, Pallas kernels for 8%

profile of v1, /device:TPU:0, one launch (start us, length us, event | category | flops | bytes accessed | tf_op | source)
XLA Modules:
  0.0 171.1 jit_solution(8310564994890326356)
XLA Ops:
  7.5 5.0 %collective-permute-start.62 = (bf16[32,1536]{1,0:T(8,128)(2,1)S(1)}, bf16[32,1536]{1,0:T(8,128)(2,1)S(1)}, u32[]{:S(2)}, u32[]{:S(2)}) collective-permute-start(bf16[32,1536]{1,0:T(8,128)(2,1)S(1)} %get-tuple-element.79), channel_id=1, source_target_pairs={{0,24},{2,26},{4,28},{6,30},{8,16},{10,18},{12,20},{14,22},{16,8},... | collective-permute-start | bytes 294920 | tf_op jit(solution)/shard_map/ppermute | solution.py:217
  13.2 3.8 %collective-permute-start.12 = (bf16[32,1536]{1,0:T(8,128)(2,1)S(1)}, bf16[32,1536]{1,0:T(8,128)(2,1)S(1)}, u32[]{:S(2)}, u32[]{:S(2)}) collective-permute-start(bf16[32,1536]{1,0:T(8,128)(2,1)S(1)} %get-tuple-element.87), channel_id=1, source_target_pairs={{0,24},{2,26},{4,28},{6,30},{8,16},{10,18},{12,20},{14,22},{16,8},... | collective-permute-start | bytes 294920 | tf_op jit(solution)/shard_map/ppermute | solution.py:217
  17.0 3.0 %collective-permute-done.51 = bf16[32,1536]{1,0:T(8,128)(2,1)S(1)} collective-permute-done((bf16[32,1536]{1,0:T(8,128)(2,1)S(1)}, bf16[32,1536]{1,0:T(8,128)(2,1)S(1)}, u32[]{:S(2)}, u32[]{:S(2)}) %collective-permute-start.51) | collective-permute-done | bytes 98336 | tf_op jit(solution)/shard_map/ppermute | solution.py:217
  20.0 2.5 %collective-permute-start.1 = (bf16[32,1536]{1,0:T(8,128)(2,1)S(1)}, bf16[32,1536]{1,0:T(8,128)(2,1)S(1)}, u32[]{:S(2)}, u32[]{:S(2)}) collective-permute-start(bf16[32,1536]{1,0:T(8,128)(2,1)S(1)} %get-tuple-element.89), channel_id=1, source_target_pairs={{0,8},{2,10},{4,12},{6,14},{8,0},{10,2},{12,4},{14,6},{16,24},{18,... | collective-permute-start | bytes 294920 | tf_op jit(solution)/shard_map/ppermute | solution.py:217
  22.5 3.7 %collective-permute-done.61 = bf16[32,1536]{1,0:T(8,128)(2,1)S(1)} collective-permute-done((bf16[32,1536]{1,0:T(8,128)(2,1)S(1)}, bf16[32,1536]{1,0:T(8,128)(2,1)S(1)}, u32[]{:S(2)}, u32[]{:S(2)}) %collective-permute-start.61) | collective-permute-done | bytes 98336 | tf_op jit(solution)/shard_map/ppermute | solution.py:217
  26.2 1.5 collective-permute-start.53
  27.7 1.6 collective-permute-start.52
  31.0 1.6 collective-permute-start.3
  33.9 1.5 collective-permute-start.2
  35.4 1.6 collective-permute-start.14
  38.1 1.5 collective-permute-start.13
  39.7 1.5 collective-permute-start.55
  45.2 1.9 %collective-permute-done.13.refs_1_ = bf16[64,1536]{1,0:T(8,128)(2,1)S(1)} collective-permute-done((bf16[64,1536]{1,0:T(8,128)(2,1)S(1)}, bf16[64,1536]{1,0:T(8,128)(2,1)S(1)}, u32[]{:S(2)}, u32[]{:S(2)}) %collective-permute-start.13) | collective-permute-done | bytes 196640 | tf_op jit(solution)/shard_map/ppermute | solution.py:208
  47.1 1.5 collective-permute-start.66
  50.2 1.7 %expert_rows.10 = (bf16[64,1536]{1,0:T(8,128)(2,1)S(1)}, bf16[64,1536]{1,0:T(8,128)(2,1)S(1)}, bf16[64,1536]{1,0:T(8,128)(2,1)S(1)}, bf16[32,1536]{1,0:T(8,128)(2,1)S(1)}, bf16[32,1536]{1,0:T(8,128)(2,1)S(1)}) custom-call(bf16[64,1536]{1,0:T(8,128)(2,1)S(1)} %pad_maximum_fusion.14.refs_0_, bf16[64,1536]{1,0:T(8,128)(2,1)S(1)} %collective-permute-done.52.refs_1_, ...), custom_call_target="tpu_custom_call" | custom-call | flops 1207959552 | bytes 6291456 | tf_op jit(solution)/shard_map/expert_rows/pallas_call | solution.py:181
  55.0 1.7 %expert_rows.11 = (bf16[64,1536]{1,0:T(8,128)(2,1)S(1)}, bf16[64,1536]{1,0:T(8,128)(2,1)S(1)}, bf16[64,1536]{1,0:T(8,128)(2,1)S(1)}, bf16[32,1536]{1,0:T(8,128)(2,1)S(1)}, bf16[32,1536]{1,0:T(8,128)(2,1)S(1)}) custom-call(bf16[64,1536]{1,0:T(8,128)(2,1)S(1)} %constant_dynamic-update-slice_fusion.4.refs_0_, ...), custom_call_target="tpu_custom_call" | custom-call | flops 1207959552 | bytes 6291456 | tf_op jit(solution)/shard_map/expert_rows/pallas_call | solution.py:181
  59.5 1.7 %expert_rows.6 = (bf16[64,1536]{1,0:T(8,128)(2,1)S(1)}, bf16[64,1536]{1,0:T(8,128)(2,1)S(1)}, bf16[64,1536]{1,0:T(8,128)(2,1)S(1)}, bf16[32,1536]{1,0:T(8,128)(2,1)S(1)}, bf16[32,1536]{1,0:T(8,128)(2,1)S(1)}) custom-call(bf16[64,1536]{1,0:T(8,128)(2,1)S(1)} %pad_maximum_fusion.refs_0_, bf16[64,1536]{1,0:T(8,128)(2,1)S(1)} %collective-permute-done.2.refs_1_, ...), custom_call_target="tpu_custom_call" | custom-call | flops 1207959552 | bytes 6291456 | tf_op jit(solution)/shard_map/expert_rows/pallas_call | solution.py:181
  63.3 1.7 %expert_rows.7 = (bf16[64,1536]{1,0:T(8,128)(2,1)S(1)}, bf16[64,1536]{1,0:T(8,128)(2,1)S(1)}, bf16[64,1536]{1,0:T(8,128)(2,1)S(1)}, bf16[32,1536]{1,0:T(8,128)(2,1)S(1)}, bf16[32,1536]{1,0:T(8,128)(2,1)S(1)}) custom-call(bf16[64,1536]{1,0:T(8,128)(2,1)S(1)} %constant_dynamic-update-slice_fusion.refs_0_, ...), custom_call_target="tpu_custom_call" | custom-call | flops 1207959552 | bytes 6291456 | tf_op jit(solution)/shard_map/expert_rows/pallas_call | solution.py:181
  68.7 1.5 collective-permute-done.69
  74.6 1.4 collective-permute-done.17
  78.8 1.7 collective-permute-done.59
  80.5 1.8 %collective-permute-start.68 = (bf16[64,1536]{1,0:T(8,128)(2,1)S(1)}, bf16[64,1536]{1,0:T(8,128)(2,1)S(1)}, u32[]{:S(2)}, u32[]{:S(2)}) collective-permute-start(bf16[64,1536]{1,0:T(8,128)(2,1)S(1)} %pad_maximum_fusion.17), channel_id=1, source_target_pairs={{0,2},{2,0},{4,6},{6,4},{8,10},{10,8},{12,14},{14,12},{16,18},{18,... | collective-permute-start | bytes 589832 | tf_op jit(solution)/shard_map/ppermute | solution.py:208
  84.2 1.5 collective-permute-done.70
  89.8 1.6 collective-permute-done.7
  91.5 1.7 %collective-permute-done.20 = bf16[64,1536]{1,0:T(8,128)(2,1)S(1)} collective-permute-done((bf16[64,1536]{1,0:T(8,128)(2,1)S(1)}, bf16[64,1536]{1,0:T(8,128)(2,1)S(1)}, u32[]{:S(2)}, u32[]{:S(2)}) %collective-permute-start.20) | collective-permute-done | bytes 196640 | tf_op jit(solution)/shard_map/ppermute | solution.py:208
  93.2 2.6 %collective-permute-start.72 = (bf16[32,1536]{1,0:T(8,128)(2,1)S(1)}, bf16[32,1536]{1,0:T(8,128)(2,1)S(1)}, u32[]{:S(2)}, u32[]{:S(2)}) collective-permute-start(bf16[32,1536]{1,0:T(8,128)(2,1)S(1)} %get-tuple-element.95), channel_id=1, source_target_pairs={{0,24},{2,26},{4,28},{6,30},{8,16},{10,18},{12,20},{14,22},{16,8},... | collective-permute-start | bytes 294920 | tf_op jit(solution)/shard_map/ppermute | solution.py:217
  97.8 1.9 %collective-permute-done.72.refs_3_ = bf16[32,1536]{1,0:T(8,128)(2,1)S(1)} collective-permute-done((bf16[32,1536]{1,0:T(8,128)(2,1)S(1)}, bf16[32,1536]{1,0:T(8,128)(2,1)S(1)}, u32[]{:S(2)}, u32[]{:S(2)}) %collective-permute-start.72) | collective-permute-done | bytes 98336 | tf_op jit(solution)/shard_map/ppermute | solution.py:217
  99.7 2.6 %collective-permute-start.22 = (bf16[32,1536]{1,0:T(8,128)(2,1)S(1)}, bf16[32,1536]{1,0:T(8,128)(2,1)S(1)}, u32[]{:S(2)}, u32[]{:S(2)}) collective-permute-start(bf16[32,1536]{1,0:T(8,128)(2,1)S(1)} %get-tuple-element.111), channel_id=1, source_target_pairs={{0,24},{2,26},{4,28},{6,30},{8,16},{10,18},{12,20},{14,22},{16,8},... | collective-permute-start | bytes 294920 | tf_op jit(solution)/shard_map/ppermute | solution.py:217
  104.3 1.9 %collective-permute-done.22.refs_3_ = bf16[32,1536]{1,0:T(8,128)(2,1)S(1)} collective-permute-done((bf16[32,1536]{1,0:T(8,128)(2,1)S(1)}, bf16[32,1536]{1,0:T(8,128)(2,1)S(1)}, u32[]{:S(2)}, u32[]{:S(2)}) %collective-permute-start.22) | collective-permute-done | bytes 98336 | tf_op jit(solution)/shard_map/ppermute | solution.py:217
  106.2 3.3 %collective-permute-done.21.refs_2_ = bf16[32,1536]{1,0:T(8,128)(2,1)S(1)} collective-permute-done((bf16[32,1536]{1,0:T(8,128)(2,1)S(1)}, bf16[32,1536]{1,0:T(8,128)(2,1)S(1)}, u32[]{:S(2)}, u32[]{:S(2)}) %collective-permute-start.21) | collective-permute-done | bytes 98336 | tf_op jit(solution)/shard_map/ppermute | solution.py:217
  109.5 1.4 collective-permute-done.23
  112.4 2.3 %shallow_end.1 = (bf16[128,1536]{1,0:T(8,128)(2,1)S(1)}, bf16[128,1536]{1,0:T(8,128)(2,1)S(1)}, f32[8,128]{1,0:T(8,128)S(1)}) custom-call(s32[3]{0:T(128)S(1)} %pad_add_fusion.scal, bf16[32,1536]{1,0:T(8,128)(2,1)S(1)} %get-tuple-element.114.refs_0_, bf16[32,1536]{1,0:T(8,128)(2,1)S(1)} %collective-permute-done.10.refs_1_, ...), custom_call_target="tpu_custom_call" | custom-call | flops 301989888 | bytes 3257356 | tf_op jit(solution)/shard_map/shallow_end/pallas_call | solution.py:181
  114.8 2.2 %collective-permute-start.38 = (bf16[32,1536]{1,0:T(8,128)(2,1)S(1)}, bf16[32,1536]{1,0:T(8,128)(2,1)S(1)}, u32[]{:S(2)}, u32[]{:S(2)}) collective-permute-start(bf16[32,1536]{1,0:T(8,128)(2,1)S(1)} %get-tuple-element.83), channel_id=1, source_target_pairs={{0,24},{2,26},{4,28},{6,30},{8,16},{10,18},{12,20},{14,22},{16,8},... | collective-permute-start | bytes 294920 | tf_op jit(solution)/shard_map/ppermute | solution.py:217
  117.0 2.3 %collective-permute-start.27 = (bf16[32,1536]{1,0:T(8,128)(2,1)S(1)}, bf16[32,1536]{1,0:T(8,128)(2,1)S(1)}, u32[]{:S(2)}, u32[]{:S(2)}) collective-permute-start(bf16[32,1536]{1,0:T(8,128)(2,1)S(1)} %get-tuple-element.85), channel_id=1, source_target_pairs={{0,8},{2,10},{4,12},{6,14},{8,0},{10,2},{12,4},{14,6},{16,24},{18,... | collective-permute-start | bytes 294920 | tf_op jit(solution)/shard_map/ppermute | solution.py:217
  119.3 5.2 %collective-permute-done.27 = bf16[32,1536]{1,0:T(8,128)(2,1)S(1)} collective-permute-done((bf16[32,1536]{1,0:T(8,128)(2,1)S(1)}, bf16[32,1536]{1,0:T(8,128)(2,1)S(1)}, u32[]{:S(2)}, u32[]{:S(2)}) %collective-permute-start.27) | collective-permute-done | bytes 98336 | tf_op jit(solution)/shard_map/ppermute | solution.py:217
  125.2 1.4 collective-permute-start.28
  128.7 3.6 %collective-permute-done.29.refs_2_ = bf16[64,1536]{1,0:T(8,128)(2,1)S(1)} collective-permute-done((bf16[64,1536]{1,0:T(8,128)(2,1)S(1)}, bf16[64,1536]{1,0:T(8,128)(2,1)S(1)}, u32[]{:S(2)}, u32[]{:S(2)}) %collective-permute-start.29) | collective-permute-done | bytes 196640 | tf_op jit(solution)/shard_map/ppermute | solution.py:208
  134.5 1.4 rest_end.1.refs_11_
  138.7 1.7 %expert_rows.8 = (bf16[64,1536]{1,0:T(8,128)(2,1)S(1)}, bf16[64,1536]{1,0:T(8,128)(2,1)S(1)}, bf16[64,1536]{1,0:T(8,128)(2,1)S(1)}, bf16[32,1536]{1,0:T(8,128)(2,1)S(1)}, bf16[32,1536]{1,0:T(8,128)(2,1)S(1)}) custom-call(bf16[64,1536]{1,0:T(8,128)(2,1)S(1)} %pad_maximum_fusion.7.refs_0_, bf16[64,1536]{1,0:T(8,128)(2,1)S(1)} %collective-permute-done.28.refs_1_, ...), custom_call_target="tpu_custom_call" | custom-call | flops 1207959552 | bytes 6291456 | tf_op jit(solution)/shard_map/expert_rows/pallas_call | solution.py:181
  140.5 1.7 %collective-permute-start.32 = (bf16[32,1536]{1,0:T(8,128)(2,1)S(1)}, bf16[32,1536]{1,0:T(8,128)(2,1)S(1)}, u32[]{:S(2)}, u32[]{:S(2)}) collective-permute-start(bf16[32,1536]{1,0:T(8,128)(2,1)S(1)} %get-tuple-element.57), channel_id=1, source_target_pairs={{0,4},{2,6},{4,0},{6,2},{8,12},{10,14},{12,8},{14,10},{16,20},{18,... | collective-permute-start | bytes 294920 | tf_op jit(solution)/shard_map/ppermute | solution.py:208
  143.4 1.7 %expert_rows.9 = (bf16[64,1536]{1,0:T(8,128)(2,1)S(1)}, bf16[64,1536]{1,0:T(8,128)(2,1)S(1)}, bf16[64,1536]{1,0:T(8,128)(2,1)S(1)}, bf16[32,1536]{1,0:T(8,128)(2,1)S(1)}, bf16[32,1536]{1,0:T(8,128)(2,1)S(1)}) custom-call(bf16[64,1536]{1,0:T(8,128)(2,1)S(1)} %constant_dynamic-update-slice_fusion.2.refs_0_, ...), custom_call_target="tpu_custom_call" | custom-call | flops 1207959552 | bytes 6291456 | tf_op jit(solution)/shard_map/expert_rows/pallas_call | solution.py:181
  148.3 1.7 %collective-permute-start.33 = (bf16[64,1536]{1,0:T(8,128)(2,1)S(1)}, bf16[64,1536]{1,0:T(8,128)(2,1)S(1)}, u32[]{:S(2)}, u32[]{:S(2)}) collective-permute-start(bf16[64,1536]{1,0:T(8,128)(2,1)S(1)} %pad_maximum_fusion.8), channel_id=1, source_target_pairs={{0,2},{2,0},{4,6},{6,4},{8,10},{10,8},{12,14},{14,12},{16,18},{18,... | collective-permute-start | bytes 589832 | tf_op jit(solution)/shard_map/ppermute | solution.py:208
  157.9 2.4 %collective-permute-start.48 = (bf16[32,1536]{1,0:T(8,128)(2,1)S(1)}, bf16[32,1536]{1,0:T(8,128)(2,1)S(1)}, u32[]{:S(2)}, u32[]{:S(2)}) collective-permute-start(bf16[32,1536]{1,0:T(8,128)(2,1)S(1)} %get-tuple-element.103), channel_id=1, source_target_pairs={{0,24},{2,26},{4,28},{6,30},{8,16},{10,18},{12,20},{14,22},{16,8},... | collective-permute-start | bytes 294920 | tf_op jit(solution)/shard_map/ppermute | solution.py:217
  160.3 1.4 collective-permute-start.47
  161.9 2.6 %collective-permute-done.48.refs_3_ = bf16[32,1536]{1,0:T(8,128)(2,1)S(1)} collective-permute-done((bf16[32,1536]{1,0:T(8,128)(2,1)S(1)}, bf16[32,1536]{1,0:T(8,128)(2,1)S(1)}, u32[]{:S(2)}, u32[]{:S(2)}) %collective-permute-start.48) | collective-permute-done | bytes 98336 | tf_op jit(solution)/shard_map/ppermute | solution.py:217
  164.5 2.9 %collective-permute-done.47.refs_2_ = bf16[32,1536]{1,0:T(8,128)(2,1)S(1)} collective-permute-done((bf16[32,1536]{1,0:T(8,128)(2,1)S(1)}, bf16[32,1536]{1,0:T(8,128)(2,1)S(1)}, u32[]{:S(2)}, u32[]{:S(2)}) %collective-permute-start.47) | collective-permute-done | bytes 98336 | tf_op jit(solution)/shard_map/ppermute | solution.py:217
  167.6 1.4 collective-permute-done.50
  169.0 2.1 %deep_end.1 = bf16[128,1536]{1,0:T(8,128)(2,1)} custom-call(s32[3]{0:T(128)S(1)} %pad_add_fusion.scal, bf16[32,1536]{1,0:T(8,128)(2,1)S(1)} %get-tuple-element.106.refs_0_, bf16[32,1536]{1,0:T(8,128)(2,1)S(1)} %collective-permute-done.36.refs_1_, bf16[32,1536]{1,0:T(8,128)(2,1)S(1)} %collective-permute-done.47.refs_2_, ...), custom_call_target="tpu_custom_call" | custom-call | flops 301989888 | bytes 2043916 | tf_op jit(solution)/shard_map/deep_end/pallas_call | solution.py:181
  (219 shorter events, 67.7 us)
Async XLA Ops:
  7.5 20.2 %collective-permute-start.62 = (bf16[32,1536]{1,0:T(8,128)(2,1)S(1)}, bf16[32,1536]{1,0:T(8,128)(2,1)S(1)}, u32[]{:S(2)}, u32[]{:S(2)}) collective-permute-start(bf16[32,1536]{1,0:T(8,128)(2,1)S(1)} %get-tuple-element.79), channel_id=1, source_target_pairs={{0,24},{2,26},{4,28},{6,30},{8,16},{10,18},{12,20},{14,22},{16,8},... | collective-permute-start | bytes 294920 | tf_op jit(solution)/shard_map/ppermute | solution.py:217
  12.5 13.6 %collective-permute-start.61 = (bf16[32,1536]{1,0:T(8,128)(2,1)S(1)}, bf16[32,1536]{1,0:T(8,128)(2,1)S(1)}, u32[]{:S(2)}, u32[]{:S(2)}) collective-permute-start(bf16[32,1536]{1,0:T(8,128)(2,1)S(1)} %get-tuple-element.80), channel_id=1, source_target_pairs={{0,16},{2,18},{4,20},{6,22},{8,24},{10,26},{12,28},{14,30},{16,0},... | collective-permute-start | bytes 294920 | tf_op jit(solution)/shard_map/ppermute | solution.py:217
  12.5 7.4 %collective-permute-start.51 = (bf16[32,1536]{1,0:T(8,128)(2,1)S(1)}, bf16[32,1536]{1,0:T(8,128)(2,1)S(1)}, u32[]{:S(2)}, u32[]{:S(2)}) collective-permute-start(bf16[32,1536]{1,0:T(8,128)(2,1)S(1)} %get-tuple-element.81), channel_id=1, source_target_pairs={{0,8},{2,10},{4,12},{6,14},{8,0},{10,2},{12,4},{14,6},{16,24},{18,... | collective-permute-start | bytes 294920 | tf_op jit(solution)/shard_map/ppermute | solution.py:217
  13.2 17.8 %collective-permute-start.12 = (bf16[32,1536]{1,0:T(8,128)(2,1)S(1)}, bf16[32,1536]{1,0:T(8,128)(2,1)S(1)}, u32[]{:S(2)}, u32[]{:S(2)}) collective-permute-start(bf16[32,1536]{1,0:T(8,128)(2,1)S(1)} %get-tuple-element.87), channel_id=1, source_target_pairs={{0,24},{2,26},{4,28},{6,30},{8,16},{10,18},{12,20},{14,22},{16,8},... | collective-permute-start | bytes 294920 | tf_op jit(solution)/shard_map/ppermute | solution.py:217
  17.0 12.8 %collective-permute-start.11 = (bf16[32,1536]{1,0:T(8,128)(2,1)S(1)}, bf16[32,1536]{1,0:T(8,128)(2,1)S(1)}, u32[]{:S(2)}, u32[]{:S(2)}) collective-permute-start(bf16[32,1536]{1,0:T(8,128)(2,1)S(1)} %get-tuple-element.88), channel_id=1, source_target_pairs={{0,16},{2,18},{4,20},{6,22},{8,24},{10,26},{12,28},{14,30},{16,0},... | collective-permute-start | bytes 294920 | tf_op jit(solution)/shard_map/ppermute | solution.py:217
  20.0 9.3 %collective-permute-start.1 = (bf16[32,1536]{1,0:T(8,128)(2,1)S(1)}, bf16[32,1536]{1,0:T(8,128)(2,1)S(1)}, u32[]{:S(2)}, u32[]{:S(2)}) collective-permute-start(bf16[32,1536]{1,0:T(8,128)(2,1)S(1)} %get-tuple-element.89), channel_id=1, source_target_pairs={{0,8},{2,10},{4,12},{6,14},{8,0},{10,2},{12,4},{14,6},{16,24},{18,... | collective-permute-start | bytes 294920 | tf_op jit(solution)/shard_map/ppermute | solution.py:217
  26.2 7.8 %collective-permute-start.53 = (bf16[64,1536]{1,0:T(8,128)(2,1)S(1)}, bf16[64,1536]{1,0:T(8,128)(2,1)S(1)}, u32[]{:S(2)}, u32[]{:S(2)}) collective-permute-start(bf16[64,1536]{1,0:T(8,128)(2,1)S(1)} %pad_maximum_fusion.14.refs_0_), channel_id=1, source_target_pairs={{0,4},{2,6},{4,0},{6,2},{8,12},{10,14},{12,8},{14,10},{16,20},{18,... | collective-permute-start | bytes 589832 | tf_op jit(solution)/shard_map/ppermute | solution.py:208
  27.7 7.7 %collective-permute-start.52 = (bf16[64,1536]{1,0:T(8,128)(2,1)S(1)}, bf16[64,1536]{1,0:T(8,128)(2,1)S(1)}, u32[]{:S(2)}, u32[]{:S(2)}) collective-permute-start(bf16[64,1536]{1,0:T(8,128)(2,1)S(1)} %pad_maximum_fusion.14.refs_0_), channel_id=1, source_target_pairs={{0,2},{2,0},{4,6},{6,4},{8,10},{10,8},{12,14},{14,12},{16,18},{18,... | collective-permute-start | bytes 589832 | tf_op jit(solution)/shard_map/ppermute | solution.py:208
  29.3 8.9 %collective-permute-start.64 = (bf16[64,1536]{1,0:T(8,128)(2,1)S(1)}, bf16[64,1536]{1,0:T(8,128)(2,1)S(1)}, u32[]{:S(2)}, u32[]{:S(2)}) collective-permute-start(bf16[64,1536]{1,0:T(8,128)(2,1)S(1)} %constant_dynamic-update-slice_fusion.4.refs_0_), channel_id=1, source_target_pairs={{0,4},{2,6},{4,0},{6,2},{8,12},{10,14},{12,8},{14,10},{16,20},{18,... | collective-permute-start | bytes 589832 | tf_op jit(solution)/shard_map/ppermute | solution.py:208
  29.9 9.8 %collective-permute-start.63 = (bf16[64,1536]{1,0:T(8,128)(2,1)S(1)}, bf16[64,1536]{1,0:T(8,128)(2,1)S(1)}, u32[]{:S(2)}, u32[]{:S(2)}) collective-permute-start(bf16[64,1536]{1,0:T(8,128)(2,1)S(1)} %constant_dynamic-update-slice_fusion.4.refs_0_), channel_id=1, source_target_pairs={{0,2},{2,0},{4,6},{6,4},{8,10},{10,8},{12,14},{14,12},{16,18},{18,... | collective-permute-start | bytes 589832 | tf_op jit(solution)/shard_map/ppermute | solution.py:208
  31.0 11.3 %collective-permute-start.3 = (bf16[64,1536]{1,0:T(8,128)(2,1)S(1)}, bf16[64,1536]{1,0:T(8,128)(2,1)S(1)}, u32[]{:S(2)}, u32[]{:S(2)}) collective-permute-start(bf16[64,1536]{1,0:T(8,128)(2,1)S(1)} %pad_maximum_fusion.refs_0_), channel_id=1, source_target_pairs={{0,4},{2,6},{4,0},{6,2},{8,12},{10,14},{12,8},{14,10},{16,20},{18,... | collective-permute-start | bytes 589832 | tf_op jit(solution)/shard_map/ppermute | solution.py:208
  33.9 9.9 %collective-permute-start.2 = (bf16[64,1536]{1,0:T(8,128)(2,1)S(1)}, bf16[64,1536]{1,0:T(8,128)(2,1)S(1)}, u32[]{:S(2)}, u32[]{:S(2)}) collective-permute-start(bf16[64,1536]{1,0:T(8,128)(2,1)S(1)} %pad_maximum_fusion.refs_0_), channel_id=1, source_target_pairs={{0,2},{2,0},{4,6},{6,4},{8,10},{10,8},{12,14},{14,12},{16,18},{18,... | collective-permute-start | bytes 589832 | tf_op jit(solution)/shard_map/ppermute | solution.py:208
  35.4 9.8 %collective-permute-start.14 = (bf16[64,1536]{1,0:T(8,128)(2,1)S(1)}, bf16[64,1536]{1,0:T(8,128)(2,1)S(1)}, u32[]{:S(2)}, u32[]{:S(2)}) collective-permute-start(bf16[64,1536]{1,0:T(8,128)(2,1)S(1)} %constant_dynamic-update-slice_fusion.refs_0_), channel_id=1, source_target_pairs={{0,4},{2,6},{4,0},{6,2},{8,12},{10,14},{12,8},{14,10},{16,20},{18,... | collective-permute-start | bytes 589832 | tf_op jit(solution)/shard_map/ppermute | solution.py:208
  38.1 9.0 %collective-permute-start.13 = (bf16[64,1536]{1,0:T(8,128)(2,1)S(1)}, bf16[64,1536]{1,0:T(8,128)(2,1)S(1)}, u32[]{:S(2)}, u32[]{:S(2)}) collective-permute-start(bf16[64,1536]{1,0:T(8,128)(2,1)S(1)} %constant_dynamic-update-slice_fusion.refs_0_), channel_id=1, source_target_pairs={{0,2},{2,0},{4,6},{6,4},{8,10},{10,8},{12,14},{14,12},{16,18},{18,... | collective-permute-start | bytes 589832 | tf_op jit(solution)/shard_map/ppermute | solution.py:208
  39.7 9.0 %collective-permute-start.55 = (bf16[32,1536]{1,0:T(8,128)(2,1)S(1)}, bf16[32,1536]{1,0:T(8,128)(2,1)S(1)}, u32[]{:S(2)}, u32[]{:S(2)}) collective-permute-start(bf16[32,1536]{1,0:T(8,128)(2,1)S(1)} %slice.319), channel_id=1, source_target_pairs={{0,2},{2,0},{4,6},{6,4},{8,10},{10,8},{12,14},{14,12},{16,18},{18,... | collective-permute-start | bytes 294920 | tf_op jit(solution)/shard_map/ppermute | solution.py:208
  42.4 6.8 %collective-permute-start.54 = (bf16[32,1536]{1,0:T(8,128)(2,1)S(1)}, bf16[32,1536]{1,0:T(8,128)(2,1)S(1)}, u32[]{:S(2)}, u32[]{:S(2)}) collective-permute-start(bf16[32,1536]{1,0:T(8,128)(2,1)S(1)} %slice.318), channel_id=1, source_target_pairs={{0,4},{2,6},{4,0},{6,2},{8,12},{10,14},{12,8},{14,10},{16,20},{18,... | collective-permute-start | bytes 294920 | tf_op jit(solution)/shard_map/ppermute | solution.py:208
  43.9 68.5 %collective-permute-start.25 = (f32[128,1536]{1,0:T(8,128)S(1)}, f32[128,1536]{1,0:T(8,128)S(1)}, u32[]{:S(2)}, u32[]{:S(2)}) collective-permute-start(f32[128,1536]{1,0:T(8,128)S(1)} %bitcast.29), channel_id=1, source_target_pairs={{0,1},{1,0},{2,3},{3,2},{4,5},{5,4},{6,7},{7,6},{8,9},{9,8},{10,11... | collective-permute-start | bytes 2359304 | tf_op jit(solution)/shard_map/ppermute | solution.py:221
  45.2 67.2 %collective-permute-start.26 = (f32[8,128]{1,0:T(8,128)S(1)}, f32[8,128]{1,0:T(8,128)S(1)}, u32[]{:S(2)}, u32[]{:S(2)}) collective-permute-start(f32[8,128]{1,0:T(8,128)S(1)} %get-tuple-element.53.refs_10_), channel_id=1, source_target_pairs={{0,1},{1,0},{2,3},{3,2},{4,5},{5,4},{6,7},{7,6},{8,9},{9,8},{10,11... | collective-permute-start | bytes 12296 | tf_op jit(solution)/shard_map/ppermute | solution.py:221
  49.1 7.7 %collective-permute-start.5 = (bf16[32,1536]{1,0:T(8,128)(2,1)S(1)}, bf16[32,1536]{1,0:T(8,128)(2,1)S(1)}, u32[]{:S(2)}, u32[]{:S(2)}) collective-permute-start(bf16[32,1536]{1,0:T(8,128)(2,1)S(1)} %slice.291), channel_id=1, source_target_pairs={{0,2},{2,0},{4,6},{6,4},{8,10},{10,8},{12,14},{14,12},{16,18},{18,... | collective-permute-start | bytes 294920 | tf_op jit(solution)/shard_map/ppermute | solution.py:208
  53.8 7.4 %collective-permute-start.16 = (bf16[32,1536]{1,0:T(8,128)(2,1)S(1)}, bf16[32,1536]{1,0:T(8,128)(2,1)S(1)}, u32[]{:S(2)}, u32[]{:S(2)}) collective-permute-start(bf16[32,1536]{1,0:T(8,128)(2,1)S(1)} %slice.297), channel_id=1, source_target_pairs={{0,2},{2,0},{4,6},{6,4},{8,10},{10,8},{12,14},{14,12},{16,18},{18,... | collective-permute-start | bytes 294920 | tf_op jit(solution)/shard_map/ppermute | solution.py:208
  58.2 6.8 %collective-permute-start.56 = (bf16[32,1536]{1,0:T(8,128)(2,1)S(1)}, bf16[32,1536]{1,0:T(8,128)(2,1)S(1)}, u32[]{:S(2)}, u32[]{:S(2)}) collective-permute-start(bf16[32,1536]{1,0:T(8,128)(2,1)S(1)} %get-tuple-element.69), channel_id=1, source_target_pairs={{0,4},{2,6},{4,0},{6,2},{8,12},{10,14},{12,8},{14,10},{16,20},{18,... | collective-permute-start | bytes 294920 | tf_op jit(solution)/shard_map/ppermute | solution.py:208
  73.2 7.3 %collective-permute-start.59 = (bf16[64,1536]{1,0:T(8,128)(2,1)S(1)}, bf16[64,1536]{1,0:T(8,128)(2,1)S(1)}, u32[]{:S(2)}, u32[]{:S(2)}) collective-permute-start(bf16[64,1536]{1,0:T(8,128)(2,1)S(1)} %pad_maximum_fusion.16), channel_id=1, source_target_pairs={{0,4},{2,6},{4,0},{6,2},{8,12},{10,14},{12,8},{14,10},{16,20},{18,... | collective-permute-start | bytes 589832 | tf_op jit(solution)/shard_map/ppermute | solution.py:208
  75.9 7.0 %collective-permute-start.57 = (bf16[64,1536]{1,0:T(8,128)(2,1)S(1)}, bf16[64,1536]{1,0:T(8,128)(2,1)S(1)}, u32[]{:S(2)}, u32[]{:S(2)}) collective-permute-start(bf16[64,1536]{1,0:T(8,128)(2,1)S(1)} %pad_maximum_fusion.15), channel_id=1, source_target_pairs={{0,2},{2,0},{4,6},{6,4},{8,10},{10,8},{12,14},{14,12},{16,18},{18,... | collective-permute-start | bytes 589832 | tf_op jit(solution)/shard_map/ppermute | solution.py:208
  78.0 7.6 %collective-permute-start.70 = (bf16[64,1536]{1,0:T(8,128)(2,1)S(1)}, bf16[64,1536]{1,0:T(8,128)(2,1)S(1)}, u32[]{:S(2)}, u32[]{:S(2)}) collective-permute-start(bf16[64,1536]{1,0:T(8,128)(2,1)S(1)} %pad_maximum_fusion.18), channel_id=1, source_target_pairs={{0,4},{2,6},{4,0},{6,2},{8,12},{10,14},{12,8},{14,10},{16,20},{18,... | collective-permute-start | bytes 589832 | tf_op jit(solution)/shard_map/ppermute | solution.py:208
  80.5 7.1 %collective-permute-start.68 = (bf16[64,1536]{1,0:T(8,128)(2,1)S(1)}, bf16[64,1536]{1,0:T(8,128)(2,1)S(1)}, u32[]{:S(2)}, u32[]{:S(2)}) collective-permute-start(bf16[64,1536]{1,0:T(8,128)(2,1)S(1)} %pad_maximum_fusion.17), channel_id=1, source_target_pairs={{0,2},{2,0},{4,6},{6,4},{8,10},{10,8},{12,14},{14,12},{16,18},{18,... | collective-permute-start | bytes 589832 | tf_op jit(solution)/shard_map/ppermute | solution.py:208
  88.6 7.1 %collective-permute-start.18 = (bf16[64,1536]{1,0:T(8,128)(2,1)S(1)}, bf16[64,1536]{1,0:T(8,128)(2,1)S(1)}, u32[]{:S(2)}, u32[]{:S(2)}) collective-permute-start(bf16[64,1536]{1,0:T(8,128)(2,1)S(1)} %pad_maximum_fusion.3), channel_id=1, source_target_pairs={{0,2},{2,0},{4,6},{6,4},{8,10},{10,8},{12,14},{14,12},{16,18},{18,... | collective-permute-start | bytes 589832 | tf_op jit(solution)/shard_map/ppermute | solution.py:208
  93.2 6.5 %collective-permute-start.72 = (bf16[32,1536]{1,0:T(8,128)(2,1)S(1)}, bf16[32,1536]{1,0:T(8,128)(2,1)S(1)}, u32[]{:S(2)}, u32[]{:S(2)}) collective-permute-start(bf16[32,1536]{1,0:T(8,128)(2,1)S(1)} %get-tuple-element.95), channel_id=1, source_target_pairs={{0,24},{2,26},{4,28},{6,30},{8,16},{10,18},{12,20},{14,22},{16,8},... | collective-permute-start | bytes 294920 | tf_op jit(solution)/shard_map/ppermute | solution.py:217
  95.8 7.5 %collective-permute-start.71 = (bf16[32,1536]{1,0:T(8,128)(2,1)S(1)}, bf16[32,1536]{1,0:T(8,128)(2,1)S(1)}, u32[]{:S(2)}, u32[]{:S(2)}) collective-permute-start(bf16[32,1536]{1,0:T(8,128)(2,1)S(1)} %get-tuple-element.96), channel_id=1, source_target_pairs={{0,16},{2,18},{4,20},{6,22},{8,24},{10,26},{12,28},{14,30},{16,0},... | collective-permute-start | bytes 294920 | tf_op jit(solution)/shard_map/ppermute | solution.py:217
  97.0 7.1 %collective-permute-start.10 = (bf16[32,1536]{1,0:T(8,128)(2,1)S(1)}, bf16[32,1536]{1,0:T(8,128)(2,1)S(1)}, u32[]{:S(2)}, u32[]{:S(2)}) collective-permute-start(bf16[32,1536]{1,0:T(8,128)(2,1)S(1)} %get-tuple-element.113), channel_id=1, source_target_pairs={{0,8},{2,10},{4,12},{6,14},{8,0},{10,2},{12,4},{14,6},{16,24},{18,... | collective-permute-start | bytes 294920 | tf_op jit(solution)/shard_map/ppermute | solution.py:217
  99.7 6.5 %collective-permute-start.22 = (bf16[32,1536]{1,0:T(8,128)(2,1)S(1)}, bf16[32,1536]{1,0:T(8,128)(2,1)S(1)}, u32[]{:S(2)}, u32[]{:S(2)}) collective-permute-start(bf16[32,1536]{1,0:T(8,128)(2,1)S(1)} %get-tuple-element.111), channel_id=1, source_target_pairs={{0,24},{2,26},{4,28},{6,30},{8,16},{10,18},{12,20},{14,22},{16,8},... | collective-permute-start | bytes 294920 | tf_op jit(solution)/shard_map/ppermute | solution.py:217
  104.2 15.1 %collective-permute-start.73 = (bf16[64,1536]{1,0:T(8,128)(2,1)S(1)}, bf16[64,1536]{1,0:T(8,128)(2,1)S(1)}, u32[]{:S(2)}, u32[]{:S(2)}) collective-permute-start(bf16[64,1536]{1,0:T(8,128)(2,1)S(1)} %pad_maximum_fusion.19), channel_id=1, source_target_pairs={{0,1},{1,0},{2,3},{3,2},{4,5},{5,4},{6,7},{7,6},{8,9},{9,8},{10,11... | collective-permute-start | bytes 589832 | tf_op jit(solution)/shard_map/ppermute | solution.py:221
  106.2 28.3 %collective-permute-start.74 = (bf16[64,1536]{1,0:T(8,128)(2,1)S(1)}, bf16[64,1536]{1,0:T(8,128)(2,1)S(1)}, u32[]{:S(2)}, u32[]{:S(2)}) collective-permute-start(bf16[64,1536]{1,0:T(8,128)(2,1)S(1)} %pad_maximum_fusion.20), channel_id=1, source_target_pairs={{0,1},{1,0},{2,3},{3,2},{4,5},{5,4},{6,7},{7,6},{8,9},{9,8},{10,11... | collective-permute-start | bytes 589832 | tf_op jit(solution)/shard_map/ppermute | solution.py:221
  114.8 11.8 %collective-permute-start.38 = (bf16[32,1536]{1,0:T(8,128)(2,1)S(1)}, bf16[32,1536]{1,0:T(8,128)(2,1)S(1)}, u32[]{:S(2)}, u32[]{:S(2)}) collective-permute-start(bf16[32,1536]{1,0:T(8,128)(2,1)S(1)} %get-tuple-element.83), channel_id=1, source_target_pairs={{0,24},{2,26},{4,28},{6,30},{8,16},{10,18},{12,20},{14,22},{16,8},... | collective-permute-start | bytes 294920 | tf_op jit(solution)/shard_map/ppermute | solution.py:217
  117.0 9.6 %collective-permute-start.37 = (bf16[32,1536]{1,0:T(8,128)(2,1)S(1)}, bf16[32,1536]{1,0:T(8,128)(2,1)S(1)}, u32[]{:S(2)}, u32[]{:S(2)}) collective-permute-start(bf16[32,1536]{1,0:T(8,128)(2,1)S(1)} %get-tuple-element.84), channel_id=1, source_target_pairs={{0,16},{2,18},{4,20},{6,22},{8,24},{10,26},{12,28},{14,30},{16,0},... | collective-permute-start | bytes 294920 | tf_op jit(solution)/shard_map/ppermute | solution.py:217
  117.0 7.5 %collective-permute-start.27 = (bf16[32,1536]{1,0:T(8,128)(2,1)S(1)}, bf16[32,1536]{1,0:T(8,128)(2,1)S(1)}, u32[]{:S(2)}, u32[]{:S(2)}) collective-permute-start(bf16[32,1536]{1,0:T(8,128)(2,1)S(1)} %get-tuple-element.85), channel_id=1, source_target_pairs={{0,8},{2,10},{4,12},{6,14},{8,0},{10,2},{12,4},{14,6},{16,24},{18,... | collective-permute-start | bytes 294920 | tf_op jit(solution)/shard_map/ppermute | solution.py:217
  124.5 7.8 %collective-permute-start.29 = (bf16[64,1536]{1,0:T(8,128)(2,1)S(1)}, bf16[64,1536]{1,0:T(8,128)(2,1)S(1)}, u32[]{:S(2)}, u32[]{:S(2)}) collective-permute-start(bf16[64,1536]{1,0:T(8,128)(2,1)S(1)} %pad_maximum_fusion.7.refs_0_), channel_id=1, source_target_pairs={{0,4},{2,6},{4,0},{6,2},{8,12},{10,14},{12,8},{14,10},{16,20},{18,... | collective-permute-start | bytes 589832 | tf_op jit(solution)/shard_map/ppermute | solution.py:208
  125.2 8.4 %collective-permute-start.28 = (bf16[64,1536]{1,0:T(8,128)(2,1)S(1)}, bf16[64,1536]{1,0:T(8,128)(2,1)S(1)}, u32[]{:S(2)}, u32[]{:S(2)}) collective-permute-start(bf16[64,1536]{1,0:T(8,128)(2,1)S(1)} %pad_maximum_fusion.7.refs_0_), channel_id=1, source_target_pairs={{0,2},{2,0},{4,6},{6,4},{8,10},{10,8},{12,14},{14,12},{16,18},{18,... | collective-permute-start | bytes 589832 | tf_op jit(solution)/shard_map/ppermute | solution.py:208
  126.6 9.9 %collective-permute-start.40 = (bf16[64,1536]{1,0:T(8,128)(2,1)S(1)}, bf16[64,1536]{1,0:T(8,128)(2,1)S(1)}, u32[]{:S(2)}, u32[]{:S(2)}) collective-permute-start(bf16[64,1536]{1,0:T(8,128)(2,1)S(1)} %constant_dynamic-update-slice_fusion.2.refs_0_), channel_id=1, source_target_pairs={{0,4},{2,6},{4,0},{6,2},{8,12},{10,14},{12,8},{14,10},{16,20},{18,... | collective-permute-start | bytes 589832 | tf_op jit(solution)/shard_map/ppermute | solution.py:208
  127.9 9.9 %collective-permute-start.39 = (bf16[64,1536]{1,0:T(8,128)(2,1)S(1)}, bf16[64,1536]{1,0:T(8,128)(2,1)S(1)}, u32[]{:S(2)}, u32[]{:S(2)}) collective-permute-start(bf16[64,1536]{1,0:T(8,128)(2,1)S(1)} %constant_dynamic-update-slice_fusion.2.refs_0_), channel_id=1, source_target_pairs={{0,2},{2,0},{4,6},{6,4},{8,10},{10,8},{12,14},{14,12},{16,18},{18,... | collective-permute-start | bytes 589832 | tf_op jit(solution)/shard_map/ppermute | solution.py:208
  132.3 6.4 %collective-permute-start.31 = (bf16[32,1536]{1,0:T(8,128)(2,1)S(1)}, bf16[32,1536]{1,0:T(8,128)(2,1)S(1)}, u32[]{:S(2)}, u32[]{:S(2)}) collective-permute-start(bf16[32,1536]{1,0:T(8,128)(2,1)S(1)} %slice.305), channel_id=1, source_target_pairs={{0,2},{2,0},{4,6},{6,4},{8,10},{10,8},{12,14},{14,12},{16,18},{18,... | collective-permute-start | bytes 294920 | tf_op jit(solution)/shard_map/ppermute | solution.py:208
  136.5 6.9 %collective-permute-start.42 = (bf16[32,1536]{1,0:T(8,128)(2,1)S(1)}, bf16[32,1536]{1,0:T(8,128)(2,1)S(1)}, u32[]{:S(2)}, u32[]{:S(2)}) collective-permute-start(bf16[32,1536]{1,0:T(8,128)(2,1)S(1)} %slice.309), channel_id=1, source_target_pairs={{0,2},{2,0},{4,6},{6,4},{8,10},{10,8},{12,14},{14,12},{16,18},{18,... | collective-permute-start | bytes 294920 | tf_op jit(solution)/shard_map/ppermute | solution.py:208
  140.5 7.8 %collective-permute-start.32 = (bf16[32,1536]{1,0:T(8,128)(2,1)S(1)}, bf16[32,1536]{1,0:T(8,128)(2,1)S(1)}, u32[]{:S(2)}, u32[]{:S(2)}) collective-permute-start(bf16[32,1536]{1,0:T(8,128)(2,1)S(1)} %get-tuple-element.57), channel_id=1, source_target_pairs={{0,4},{2,6},{4,0},{6,2},{8,12},{10,14},{12,8},{14,10},{16,20},{18,... | collective-permute-start | bytes 294920 | tf_op jit(solution)/shard_map/ppermute | solution.py:208
  145.2 6.8 %collective-permute-start.43 = (bf16[32,1536]{1,0:T(8,128)(2,1)S(1)}, bf16[32,1536]{1,0:T(8,128)(2,1)S(1)}, u32[]{:S(2)}, u32[]{:S(2)}) collective-permute-start(bf16[32,1536]{1,0:T(8,128)(2,1)S(1)} %get-tuple-element.62), channel_id=1, source_target_pairs={{0,4},{2,6},{4,0},{6,2},{8,12},{10,14},{12,8},{14,10},{16,20},{18,... | collective-permute-start | bytes 294920 | tf_op jit(solution)/shard_map/ppermute | solution.py:208
  148.0 6.6 %collective-permute-start.35 = (bf16[64,1536]{1,0:T(8,128)(2,1)S(1)}, bf16[64,1536]{1,0:T(8,128)(2,1)S(1)}, u32[]{:S(2)}, u32[]{:S(2)}) collective-permute-start(bf16[64,1536]{1,0:T(8,128)(2,1)S(1)} %pad_maximum_fusion.9), channel_id=1, source_target_pairs={{0,4},{2,6},{4,0},{6,2},{8,12},{10,14},{12,8},{14,10},{16,20},{18,... | collective-permute-start | bytes 589832 | tf_op jit(solution)/shard_map/ppermute | solution.py:208
  148.3 6.7 %collective-permute-start.33 = (bf16[64,1536]{1,0:T(8,128)(2,1)S(1)}, bf16[64,1536]{1,0:T(8,128)(2,1)S(1)}, u32[]{:S(2)}, u32[]{:S(2)}) collective-permute-start(bf16[64,1536]{1,0:T(8,128)(2,1)S(1)} %pad_maximum_fusion.8), channel_id=1, source_target_pairs={{0,2},{2,0},{4,6},{6,4},{8,10},{10,8},{12,14},{14,12},{16,18},{18,... | collective-permute-start | bytes 589832 | tf_op jit(solution)/shard_map/ppermute | solution.py:208
  155.2 6.6 %collective-permute-start.36 = (bf16[32,1536]{1,0:T(8,128)(2,1)S(1)}, bf16[32,1536]{1,0:T(8,128)(2,1)S(1)}, u32[]{:S(2)}, u32[]{:S(2)}) collective-permute-start(bf16[32,1536]{1,0:T(8,128)(2,1)S(1)} %get-tuple-element.105), channel_id=1, source_target_pairs={{0,8},{2,10},{4,12},{6,14},{8,0},{10,2},{12,4},{14,6},{16,24},{18,... | collective-permute-start | bytes 294920 | tf_op jit(solution)/shard_map/ppermute | solution.py:217
  157.9 6.6 %collective-permute-start.48 = (bf16[32,1536]{1,0:T(8,128)(2,1)S(1)}, bf16[32,1536]{1,0:T(8,128)(2,1)S(1)}, u32[]{:S(2)}, u32[]{:S(2)}) collective-permute-start(bf16[32,1536]{1,0:T(8,128)(2,1)S(1)} %get-tuple-element.103), channel_id=1, source_target_pairs={{0,24},{2,26},{4,28},{6,30},{8,16},{10,18},{12,20},{14,22},{16,8},... | collective-permute-start | bytes 294920 | tf_op jit(solution)/shard_map/ppermute | solution.py:217
  160.3 7.1 %collective-permute-start.47 = (bf16[32,1536]{1,0:T(8,128)(2,1)S(1)}, bf16[32,1536]{1,0:T(8,128)(2,1)S(1)}, u32[]{:S(2)}, u32[]{:S(2)}) collective-permute-start(bf16[32,1536]{1,0:T(8,128)(2,1)S(1)} %get-tuple-element.104), channel_id=1, source_target_pairs={{0,16},{2,18},{4,20},{6,22},{8,24},{10,26},{12,28},{14,30},{16,0},... | collective-permute-start | bytes 294920 | tf_op jit(solution)/shard_map/ppermute | solution.py:217
  (37 other events, 329.3 us)

commit v2 on v1

--- a/solution.py
+++ b/solution.py
@@ -45,19 +45,23 @@
         per_expert = jnp.where(first, weights[0:1], jnp.where(second, weights[1:2], 0.0))
         columns.extend(pieces3(per_expert))
     table = jnp.concatenate(columns, axis=1)
-    rows = 2 * experts * half
+    rows, mine = 2 * experts * half, experts * half
     slot = lax.broadcasted_iota(jnp.int32, (rows, padded), 0)
-    block = jnp.where(slot >= experts * half, slot - experts * half, slot)
     owner = lax.broadcasted_iota(jnp.int32, (rows, padded), 1)
-    spread = (block >= owner * half) & (block < (owner + 1) * half)
+    side = jnp.where(slot >= mine, 1 - core, core)
+    block = jnp.where(slot >= mine, slot - mine, slot)
+    split = owner < 2
+    low = jnp.where(split, owner * half, (owner >> 1) * (2 * half))
+    high = low + jnp.where(split, half, 2 * half)
+    spread = (block >= low) & (block < high) & (split | ((owner & 1) == side))
     wide = jnp.dot(jnp.where(spread, 1.0, 0.0).astype(BF), table, preferred_element_type=F32)
     slot = lax.broadcasted_iota(jnp.int32, (rows, tokens), 0)
-    other = slot >= experts * half
-    block = jnp.where(other, slot - experts * half, slot)
-    within = block
-    for step in range(1, experts):
-        within = within - jnp.where(block >= step * half, half, 0)
-    within = within + jnp.where(other, (1 - core) * half, core * half)
+    side = jnp.where(slot >= mine, 1 - core, core)
+    block = jnp.where(slot >= mine, slot - mine, slot)
+    within = block + jnp.where(block < 2 * half, side * half, 0)
+    within = within - jnp.where((block >= half) & (block < 2 * half), half, 0)
+    for step in range(1, experts // 2):
+        within = within - jnp.where(block >= step * 2 * half, 2 * half, 0)
     taken = wide[:, :tokens] == within.astype(F32)
     if weights is None:
         return jnp.where(taken, 1.0, 0.0).astype(BF)
@@ -105,7 +109,7 @@
 
 def pre_kernel(experts, half, scal, feats, mod, routes, router_t, keep, send, pack):
     home, core = scal[0], scal[1]
-    normed = normalise(feats[...], mod[core, 0:1, :], mod[core, 1:2, :])
+    normed = normalise(feats[...], mod[0, pl.ds(core, 1), :], mod[1, pl.ds(core, 1), :])
     onehot = slot_rows(routes[...], None, home, core, experts, half)
     rows = jnp.dot(onehot, normed, preferred_element_type=F32).astype(BF)
     keep[...] = rows[: experts * half]
@@ -128,9 +132,9 @@
     gather_blocks(scratch, blocks)
     moe = mixed(scratch, jnp.where(is_root, pack[...], pack_o[...]), home, core, experts, half)
     features = jnp.where(is_root, feats[...], feats_o[...])
-    shallow = (features + mod[root, 2:3, :] * moe).astype(BF)
+    shallow = (features + mod[2, pl.ds(root, 1), :] * moe).astype(BF)
     after[...] = shallow
-    normed = normalise(shallow.astype(F32), mod[root, 3:4, :], mod[root, 4:5, :])
+    normed = normalise(shallow.astype(F32), mod[3, pl.ds(root, 1), :], mod[4, pl.ds(root, 1), :])
     onehot = slot_rows(routes[...], None, home, core, experts, half)[: experts * half]
     keep[...] = jnp.dot(onehot, normed, preferred_element_type=F32).astype(BF)
     pack_out[...] = gate_pack(normed, routes[...], padded_router(router_t, experts), experts)
@@ -144,7 +148,7 @@
     gather_blocks(scratch, blocks)
     moe = mixed(scratch, jnp.where(is_root, pack_o[...], pack[...]), home, core, experts, half)
     features = jnp.where(is_root, feats_o[...], feats[...])
-    after[...] = (features + mod[1 - root, 2:3, :] * moe).astype(BF)
+    after[...] = (features + mod[2, pl.ds(1 - root, 1), :] * moe).astype(BF)
 
 
 def last_kernel(experts, half, n_blocks, scal, *refs):
@@ -153,7 +157,7 @@
     home, core, root = scal[0], scal[1], scal[2]
     gather_blocks(scratch, blocks)
     moe = mixed(scratch, pack[...], home, core, experts, half)
-    delta = (mod[root, 5:6, :] * moe).astype(BF)
+    delta = (mod[5, pl.ds(root, 1), :] * moe).astype(BF)
     mine = jnp.where(core == root, after_root[...].astype(F32), after_rest[...].astype(F32))
     result[...] = (mine + delta.astype(F32)).astype(BF)
 
@@ -198,23 +202,26 @@
     def __init__(self, experts, quarters):
         self.experts, self.quarters = experts, quarters
 
-    def plane(self, value, turn):
-        quarters = self.quarters
-        pairs = [
-            (e * quarters + q, e * quarters + (q ^ turn))
-            for e in range(self.experts)
-            for q in range(quarters)
-        ]
-        return lax.ppermute(value, "expert", pairs)
-
-    def far(self, value, turn):
-        quarters = self.quarters
-        pairs = [
-            (e * quarters + q, (e ^ turn) * quarters + q)
-            for e in range(self.experts)
-            for q in range(quarters)
-        ]
-        return lax.ppermute(value, "expert", pairs)
+    def send(self, value, turns):
+        pairs = []
+        for e in range(self.experts):
+            for q in range(self.quarters):
+                for c, (far, near) in enumerate(turns):
+                    target = (e ^ far) * self.quarters + (q ^ near)
+                    pairs.append(((e * self.quarters + q) * 2 + c, target * 2 + c))
+        return lax.ppermute(value, ("expert", "step"), pairs)
+
+    def first(self, value):
+        return self.send(value, ((0, 1), (0, 2)))
+
+    def second(self, value):
+        return self.send(value, ((0, 2), (0, 1)))
+
+    def close(self, value):
+        return self.send(value, ((1, 0), (1, 0)))
+
+    def far(self, value, pair):
+        return self.send(value, ((2 * pair, 0), (2 * pair + 1, 0)))
 
 
 def swap(value):
@@ -235,48 +242,63 @@
     )
 
 
-def layer_half(rows, half, w_in, w_out, links, groups):
-    experts = links.experts
-    arrived = {}
-    for turn in range(experts):
-        block = rows[turn * half : (turn + 1) * half]
-        arrived[turn] = links.far(block, turn) if turn else block
-    back = {}
-    for group in groups:
-        mine = jnp.concatenate([arrived[t] for t in group], axis=0)
-        cut = mine.shape[0] // 2
-        from_x = links.plane(mine, 1)
-        from_y = links.plane(mine, 2)
-        diag_a = links.plane(from_x[:cut], 2)
-        diag_b = links.plane(from_y[cut:], 1)
-        own, px, py, pa, pb = expert_call([mine, from_x, from_y, diag_a, diag_b], w_in, w_out)
-        via_y = links.plane(pa, 2)
-        via_x = links.plane(pb, 1)
-        to_x = jnp.concatenate(
-            [(px[:cut].astype(F32) + via_y.astype(F32)).astype(BF), px[cut:]], axis=0
-        )
-        to_y = jnp.concatenate(
-            [py[:cut], (py[cut:].astype(F32) + via_x.astype(F32)).astype(BF)], axis=0
-        )
-        total = (
-            own.astype(F32)
-            + links.plane(to_x, 1).astype(F32)
-            + links.plane(to_y, 2).astype(F32)
-        ).astype(BF)
-        for k, turn in enumerate(group):
-            block = total[k * half : (k + 1) * half]
-            back[turn] = links.far(block, turn) if turn else block
-    return [back[t] for t in range(experts)]
-
-
-def both_cores(blocks, groups):
-    other = {}
-    for group in groups:
-        joined = swap(jnp.concatenate([blocks[t] for t in group], axis=0))
-        size = joined.shape[0] // len(group)
-        for k, t in enumerate(group):
-            other[t] = joined[k * size : (k + 1) * size]
-    return blocks + [other[t] for t in range(len(blocks))]
+def tie(value, *others):
+    return lax.optimization_barrier((value, *others))[0]
+
+
+def add(*values):
+    total = values[0].astype(F32)
+    for value in values[1:]:
+        total = total + value.astype(F32)
+    return total.astype(BF)
+
+
+class Stage:
+    def __init__(self, links, half, w_in, w_out):
+        self.links, self.half, self.w_in, self.w_out = links, half, w_in, w_out
+
+    def out_close(self, rows):
+        half = self.half
+        return jnp.concatenate([rows[:half], self.links.close(rows[half : 2 * half])], axis=0)
+
+    def out_far(self, rows):
+        half = self.half
+        pairs = self.links.experts // 2
+        blocks = [
+            self.links.far(rows[2 * half * k : 2 * half * (k + 1)], k) for k in range(1, pairs)
+        ]
+        return blocks[0] if len(blocks) == 1 else jnp.concatenate(blocks, axis=0)
+
+    def step1(self, chunk):
+        return self.links.first(chunk)
+
+    def step2(self, chunk, near):
+        return self.links.second(jnp.concatenate([chunk, near], axis=0))
+
+    def experts(self, chunk, near, wide):
+        return expert_call([chunk, near, wide], self.w_in, self.w_out)
+
+    def back1(self, wide):
+        return self.links.second(wide)
+
+    def back2(self, near, wide):
+        size = near.shape[0]
+        return self.links.first(add(near, wide[size:]))
+
+    def total(self, own, wide, near):
+        return add(own, wide[: own.shape[0]], near)
+
+    def home_close(self, total):
+        half = self.half
+        return jnp.concatenate([total[:half], self.links.close(total[half:])], axis=0)
+
+    def home_far(self, total):
+        half = self.half
+        blocks = [
+            self.links.far(total[2 * half * k : 2 * half * (k + 1)], k + 1)
+            for k in range(total.shape[0] // (2 * half))
+        ]
+        return blocks[0] if len(blocks) == 1 else jnp.concatenate(blocks, axis=0)
 
 
 def body(
@@ -305,10 +327,8 @@
     is_root = core == root
     slots = experts * half
     partial = functools.partial
-    cut = experts // 2
-    groups = [list(range(cut)), list(range(cut, experts))]
-
     feats = latents[0]
+    modulation = modulation.transpose(1, 0, 2)
     keep, send, pack = call(
         partial(pre_kernel, experts, half),
         [struct((slots, width), BF), struct((slots, width), BF), struct((8, tokens), F32)],
@@ -325,8 +345,36 @@
     scratch = [pltpu.VMEM((2 * slots, width), BF)]
     mix_flops = 12 * slots * tokens * width
 
-    back_root = layer_half(rows_root, half, shallow_in[0], shallow_out[0], links, groups)
-    blocks = both_cores(back_root, groups)
+    one = Stage(links, half, shallow_in[0], shallow_out[0])
+    two = Stage(links, half, shallow_in[0], shallow_out[0])
+    three = Stage(links, half, deep_in[0], deep_out[0])
+
+    a_far = one.out_far(rows_root)
+    a_close = one.out_close(rows_root)
+    a_near1 = one.step1(a_close)
+    a_wide1 = one.step2(a_close, a_near1)
+    a_near2 = one.step1(a_far)
+    a_wide2 = one.step2(a_far, a_near2)
+    b_close = two.out_close(rows_rest)
+    b_far = two.out_far(tie(rows_rest, a_far))
+    b_close = tie(b_close, a_near1)
+    b_near1 = two.step1(b_close)
+    b_wide1 = two.step2(b_close, b_near1)
+    a_own1, a_n1, a_w1 = one.experts(a_close, a_near1, a_wide1)
+    a_own2, a_n2, a_w2 = one.experts(a_far, a_near2, a_wide2)
+    a_bw2 = one.back1(a_w2)
+    a_bn2 = one.back2(a_n2, a_bw2)
+    a_total2 = one.total(a_own2, a_bw2, a_bn2)
+    a_home2 = one.home_far(a_total2)
+    a_bw1 = one.back1(a_w1)
+    a_bn1 = one.back2(a_n1, a_bw1)
+    a_home1 = one.home_close(one.total(a_own1, a_bw1, a_bn1))
+    b_far = tie(b_far, a_total2)
+    b_near2 = two.step1(b_far)
+    b_wide2 = two.step2(b_far, b_near2)
+    b_own1, b_n1, b_w1 = two.experts(b_close, b_near1, b_wide1)
+    b_own2, b_n2, b_w2 = two.experts(b_far, b_near2, b_wide2)
+    blocks = [a_home1, a_home2, swap(a_home1), swap(a_home2)]
     after_root, rows_deep, pack_deep = call(
         partial(mid_kernel, experts, half, len(blocks)),
         [struct((tokens, width), BF), struct((slots, width), BF), struct((8, tokens), F32)],
@@ -335,8 +383,19 @@
         mix_flops,
         "shallow_end",
     )
-    back_rest = layer_half(rows_rest, half, shallow_in[0], shallow_out[0], links, groups)
-    blocks = both_cores(back_rest, groups)
+    c_far = three.out_far(rows_deep)
+    c_close = three.out_close(rows_deep)
+    c_near1 = three.step1(c_close)
+    c_wide1 = three.step2(c_close, c_near1)
+    c_near2 = three.step1(c_far)
+    c_wide2 = three.step2(c_far, c_near2)
+    b_bw1 = two.back1(tie(b_w1, a_total2))
+    b_bn1 = two.back2(b_n1, b_bw1)
+    b_bw2 = two.back1(tie(b_w2, rows_deep))
+    b_bn2 = two.back2(b_n2, b_bw2)
+    b_home1 = two.home_close(two.total(b_own1, b_bw1, b_bn1))
+    b_home2 = two.home_far(tie(two.total(b_own2, b_bw2, b_bn2), c_far))
+    blocks = [b_home1, b_home2, swap(b_home1), swap(b_home2)]
     (after_rest,) = call(
         partial(rest_kernel, experts, half, len(blocks)),
         [struct((tokens, width), BF)],
@@ -345,8 +404,15 @@
         mix_flops,
         "rest_end",
     )
-    back_deep = layer_half(rows_deep, half, deep_in[0], deep_out[0], links, groups)
-    blocks = both_cores(back_deep, groups)
+    c_own1, c_n1, c_w1 = three.experts(c_close, c_near1, c_wide1)
+    c_own2, c_n2, c_w2 = three.experts(c_far, c_near2, c_wide2)
+    c_bw2 = three.back1(c_w2)
+    c_bn2 = three.back2(c_n2, c_bw2)
+    c_home2 = three.home_far(three.total(c_own2, c_bw2, c_bn2))
+    c_bw1 = three.back1(c_w1)
+    c_bn1 = three.back2(c_n1, c_bw1)
+    c_home1 = three.home_close(three.total(c_own1, c_bw1, c_bn1))
+    blocks = [c_home1, c_home2, swap(c_home1), swap(c_home2)]
     (result,) = call(
         partial(last_kernel, experts, half, len(blocks)),
         [struct((tokens, width), BF)],

time: 171 us -> 138 us (0.81)
  starting transfers between devices: 81.6 us -> 62.2 us
  waiting for transfers between devices: 65.4 us -> 51.9 us
    ppermute x66 -> x36, starting transfers between devices: 80.6 us -> 61 us  [send(): return lax.ppermute(value, ('expert', 'step'), pairs)]
    ppermute x66 -> x36, waiting for transfers between devices: 60 us -> 50.5 us  [send(): return lax.ppermute(value, ('expert', 'step'), pairs)]
    ppermute x9, waiting for transfers between devices: 5.46 us -> 1.41 us  [swap(): return lax.ppermute(value, 'step', [(0, 1), (1, 0)])]
  transfers between devices with their start and end apart: 75 -> 45, of which waited for: 45 -> 23; matrix products, arithmetic and copies ran while one was open for 1% -> 1% of each run, Pallas kernels for 8% -> 10%
where the time goes in v2:
time: 138 us; the launch traced here: 137 us
  starting transfers between devices  62.2 us (45%)
  waiting for transfers between devices  51.9 us (38%)
  Pallas kernels  17.3 us (13%)
  local copies, waits for them, and re-layouts  3.62 us (3%)
    ppermute x36, starting transfers between devices, send(): return lax.ppermute(value, ('expert', 'step'), pairs)  61 us
    ppermute x36, waiting for transfers between devices, send(): return lax.ppermute(value, ('expert', 'step'), pairs)  50.5 us
    pallas_call x10, Pallas kernels, call(): pl.pallas_call(kernel, out_shape=outs, in_specs=specs, out_specs=[pl.Bloc...  17.3 us
    unnamed x24, local copies, waits for them, and re-layouts  3.48 us
  transfers between devices with their start and end apart: 45, of which 23 were waited for; matrix products, arithmetic and copies ran while one was open for 1% of the time, Pallas kernels for 10%

profile of v2, /device:TPU:0, one launch (start us, length us, event | category | flops | bytes accessed | tf_op | source)
XLA Modules:
  0.0 137.4 jit_solution(5887699680603709131)
XLA Ops:
  0.7 1.1 copy-done.4
  4.2 1.3 shallow_start.1
  6.0 1.3 collective-permute-done
  7.5 4.0 %collective-permute-start.7 = (bf16[64,1536]{1,0:T(8,128)(2,1)S(1)}, bf16[64,1536]{1,0:T(8,128)(2,1)S(1)}, u32[]{:S(2)}, u32[]{:S(2)}) collective-permute-start(bf16[64,1536]{1,0:T(8,128)(2,1)S(1)} %slice.114), channel_id=1, source_target_pairs={{0,16},{1,25},{2,18},{3,27},{4,20},{5,29},{6,22},{7,31},{8,24},{9,... | collective-permute-start | bytes 589832 | tf_op jit(solution)/shard_map/ppermute | solution.py:212
  11.5 1.6 %collective-permute-start.1 = (bf16[32,1536]{1,0:T(8,128)(2,1)S(1)}, bf16[32,1536]{1,0:T(8,128)(2,1)S(1)}, u32[]{:S(2)}, u32[]{:S(2)}) collective-permute-start(bf16[32,1536]{1,0:T(8,128)(2,1)S(1)} %get-tuple-element.72), channel_id=1, source_target_pairs={{0,8},{1,9},{2,10},{3,11},{4,12},{5,13},{6,14},{7,15},{8,0},{9,1},... | collective-permute-start | bytes 294920 | tf_op jit(solution)/shard_map/ppermute | solution.py:212
  13.6 5.2 %collective-permute-done.1 = bf16[32,1536]{1,0:T(8,128)(2,1)S(1)} collective-permute-done((bf16[32,1536]{1,0:T(8,128)(2,1)S(1)}, bf16[32,1536]{1,0:T(8,128)(2,1)S(1)}, u32[]{:S(2)}, u32[]{:S(2)}) %collective-permute-start.1) | collective-permute-done | bytes 98336 | tf_op jit(solution)/shard_map/ppermute | solution.py:212
  18.8 1.6 %collective-permute-start.2 = (bf16[64,1536]{1,0:T(8,128)(2,1)S(1)}, bf16[64,1536]{1,0:T(8,128)(2,1)S(1)}, u32[]{:S(2)}, u32[]{:S(2)}) collective-permute-start(bf16[64,1536]{1,0:T(8,128)(2,1)S(1)} %pad_maximum_fusion.6.refs_0_), channel_id=1, source_target_pairs={{0,2},{1,5},{2,0},{3,7},{4,6},{5,1},{6,4},{7,3},{8,10},{9,13},{10,... | collective-permute-start | bytes 589832 | tf_op jit(solution)/shard_map/ppermute | solution.py:212
  20.3 1.7 %collective-permute-done.31 = bf16[32,1536]{1,0:T(8,128)(2,1)S(1)} collective-permute-done((bf16[32,1536]{1,0:T(8,128)(2,1)S(1)}, bf16[32,1536]{1,0:T(8,128)(2,1)S(1)}, u32[]{:S(2)}, u32[]{:S(2)}) %collective-permute-start.31) | collective-permute-done | bytes 98336 | tf_op jit(solution)/shard_map/ppermute | solution.py:212
  22.0 1.7 %collective-permute-start.8 = (bf16[64,1536]{1,0:T(8,128)(2,1)S(1)}, bf16[64,1536]{1,0:T(8,128)(2,1)S(1)}, u32[]{:S(2)}, u32[]{:S(2)}) collective-permute-start(bf16[64,1536]{1,0:T(8,128)(2,1)S(1)} %collective-permute-done.7.refs_0_), channel_id=1, source_target_pairs={{0,2},{1,5},{2,0},{3,7},{4,6},{5,1},{6,4},{7,3},{8,10},{9,13},{10,... | collective-permute-start | bytes 589832 | tf_op jit(solution)/shard_map/ppermute | solution.py:212
  24.5 1.6 %collective-permute-start.3 = (bf16[128,1536]{1,0:T(8,128)(2,1)S(1)}, bf16[128,1536]{1,0:T(8,128)(2,1)S(1)}, u32[]{:S(2)}, u32[]{:S(2)}) collective-permute-start(bf16[128,1536]{1,0:T(8,128)(2,1)S(1)} %pad_maximum_fusion), channel_id=1, source_target_pairs={{0,4},{1,3},{2,6},{3,1},{4,0},{5,7},{6,2},{7,5},{8,12},{9,11},{10,... | collective-permute-start | bytes 1179656 | tf_op jit(solution)/shard_map/ppermute | solution.py:212
  26.1 1.5 %collective-permute-start.32 = (bf16[64,1536]{1,0:T(8,128)(2,1)S(1)}, bf16[64,1536]{1,0:T(8,128)(2,1)S(1)}, u32[]{:S(2)}, u32[]{:S(2)}) collective-permute-start(bf16[64,1536]{1,0:T(8,128)(2,1)S(1)} %pad_maximum_fusion.10.refs_0_), channel_id=1, source_target_pairs={{0,2},{1,5},{2,0},{3,7},{4,6},{5,1},{6,4},{7,3},{8,10},{9,13},{10,... | collective-permute-start | bytes 589832 | tf_op jit(solution)/shard_map/ppermute | solution.py:212
  28.7 1.9 %collective-permute-start.9 = (bf16[128,1536]{1,0:T(8,128)(2,1)S(1)}, bf16[128,1536]{1,0:T(8,128)(2,1)S(1)}, u32[]{:S(2)}, u32[]{:S(2)}) collective-permute-start(bf16[128,1536]{1,0:T(8,128)(2,1)S(1)} %pad_maximum_fusion.1), channel_id=1, source_target_pairs={{0,4},{1,3},{2,6},{3,1},{4,0},{5,7},{6,2},{7,5},{8,12},{9,11},{10,... | collective-permute-start | bytes 1179656 | tf_op jit(solution)/shard_map/ppermute | solution.py:212
  30.6 3.3 %collective-permute-done.32.refs_1_ = bf16[64,1536]{1,0:T(8,128)(2,1)S(1)} collective-permute-done((bf16[64,1536]{1,0:T(8,128)(2,1)S(1)}, bf16[64,1536]{1,0:T(8,128)(2,1)S(1)}, u32[]{:S(2)}, u32[]{:S(2)}) %collective-permute-start.32) | collective-permute-done | bytes 196640 | tf_op jit(solution)/shard_map/ppermute | solution.py:212
  34.9 1.7 %expert_rows.6 = (bf16[64,1536]{1,0:T(8,128)(2,1)S(1)}, bf16[64,1536]{1,0:T(8,128)(2,1)S(1)}, bf16[128,1536]{1,0:T(8,128)(2,1)S(1)}) custom-call(bf16[64,1536]{1,0:T(8,128)(2,1)S(1)} %pad_maximum_fusion.6.refs_0_, bf16[64,1536]{1,0:T(8,128)(2,1)S(1)} %collective-permute-done.2.refs_1_, bf16[128,1536]{1,0:T(8,128)(2,1)S(1)} %collective-permute-done.3.refs_2_, ...), custom_call_target="tpu_custom_call" | custom-call | flops 1207959552 | bytes 6291456 | tf_op jit(solution)/shard_map/expert_rows/pallas_call | solution.py:185
  36.6 1.3 collective-permute-start.4
  38.6 2.6 %collective-permute-start.37 = (bf16[64,1536]{1,0:T(8,128)(2,1)S(1)}, bf16[64,1536]{1,0:T(8,128)(2,1)S(1)}, u32[]{:S(2)}, u32[]{:S(2)}) collective-permute-start(bf16[64,1536]{1,0:T(8,128)(2,1)S(1)} %slice.105), channel_id=1, source_target_pairs={{0,16},{1,25},{2,18},{3,27},{4,20},{5,29},{6,22},{7,31},{8,24},{9,... | collective-permute-start | bytes 589832 | tf_op jit(solution)/shard_map/ppermute | solution.py:212
  41.1 1.7 %expert_rows.7 = (bf16[64,1536]{1,0:T(8,128)(2,1)S(1)}, bf16[64,1536]{1,0:T(8,128)(2,1)S(1)}, bf16[128,1536]{1,0:T(8,128)(2,1)S(1)}) custom-call(bf16[64,1536]{1,0:T(8,128)(2,1)S(1)} %collective-permute-done.7.refs_0_, bf16[64,1536]{1,0:T(8,128)(2,1)S(1)} %collective-permute-done.8.refs_1_, bf16[128,1536]{1,0:T(8,128)(2,1)S(1)} %collective-permute-done.9.refs_2_, ...), custom_call_target="tpu_custom_call" | custom-call | flops 1207959552 | bytes 6291456 | tf_op jit(solution)/shard_map/expert_rows/pallas_call | solution.py:185
  42.9 1.4 %collective-permute-start.10 = (bf16[128,1536]{1,0:T(8,128)(2,1)S(1)}, bf16[128,1536]{1,0:T(8,128)(2,1)S(1)}, u32[]{:S(2)}, u32[]{:S(2)}) collective-permute-start(bf16[128,1536]{1,0:T(8,128)(2,1)S(1)} %get-tuple-element.41), channel_id=1, source_target_pairs={{0,4},{1,3},{2,6},{3,1},{4,0},{5,7},{6,2},{7,5},{8,12},{9,11},{10,... | collective-permute-start | bytes 1179656 | tf_op jit(solution)/shard_map/ppermute | solution.py:212
  44.3 1.7 %expert_rows.10 = (bf16[64,1536]{1,0:T(8,128)(2,1)S(1)}, bf16[64,1536]{1,0:T(8,128)(2,1)S(1)}, bf16[128,1536]{1,0:T(8,128)(2,1)S(1)}) custom-call(bf16[64,1536]{1,0:T(8,128)(2,1)S(1)} %pad_maximum_fusion.10.refs_0_, bf16[64,1536]{1,0:T(8,128)(2,1)S(1)} %collective-permute-done.32.refs_1_, bf16[128,1536]{1,0:T(8,128)(2,1)S(1)} %collective-permute-done.33.refs_2_, ...), custom_call_target="tpu_custom_call" | custom-call | flops 1207959552 | bytes 6291456 | tf_op jit(solution)/shard_map/expert_rows/pallas_call | solution.py:185
  47.6 5.2 %collective-permute-done.10 = bf16[128,1536]{1,0:T(8,128)(2,1)S(1)} collective-permute-done((bf16[128,1536]{1,0:T(8,128)(2,1)S(1)}, bf16[128,1536]{1,0:T(8,128)(2,1)S(1)}, u32[]{:S(2)}, u32[]{:S(2)}) %collective-permute-start.10) | collective-permute-done | bytes 393248 | tf_op jit(solution)/shard_map/ppermute | solution.py:212
  53.5 3.1 %collective-permute-start.6 = (bf16[32,1536]{1,0:T(8,128)(2,1)S(1)}, bf16[32,1536]{1,0:T(8,128)(2,1)S(1)}, u32[]{:S(2)}, u32[]{:S(2)}) collective-permute-start(bf16[32,1536]{1,0:T(8,128)(2,1)S(1)} %get-tuple-element.78), channel_id=1, source_target_pairs={{0,8},{1,9},{2,10},{3,11},{4,12},{5,13},{6,14},{7,15},{8,0},{9,1},... | collective-permute-start | bytes 294920 | tf_op jit(solution)/shard_map/ppermute | solution.py:212
  56.6 2.1 %collective-permute-done.11 = bf16[64,1536]{1,0:T(8,128)(2,1)S(1)} collective-permute-done((bf16[64,1536]{1,0:T(8,128)(2,1)S(1)}, bf16[64,1536]{1,0:T(8,128)(2,1)S(1)}, u32[]{:S(2)}, u32[]{:S(2)}) %collective-permute-start.11) | collective-permute-done | bytes 196640 | tf_op jit(solution)/shard_map/ppermute | solution.py:212
  58.7 1.9 %collective-permute-start.12 = (bf16[64,1536]{1,0:T(8,128)(2,1)S(1)}, bf16[64,1536]{1,0:T(8,128)(2,1)S(1)}, u32[]{:S(2)}, u32[]{:S(2)}) collective-permute-start(bf16[64,1536]{1,0:T(8,128)(2,1)S(1)} %add_convert_fusion.8), channel_id=1, source_target_pairs={{0,16},{1,25},{2,18},{3,27},{4,20},{5,29},{6,22},{7,31},{8,24},{9,... | collective-permute-start | bytes 589832 | tf_op jit(solution)/shard_map/ppermute | solution.py:212
  60.7 1.5 %collective-permute-start.38 = (bf16[64,1536]{1,0:T(8,128)(2,1)S(1)}, bf16[64,1536]{1,0:T(8,128)(2,1)S(1)}, u32[]{:S(2)}, u32[]{:S(2)}) collective-permute-start(bf16[64,1536]{1,0:T(8,128)(2,1)S(1)} %collective-permute-done.37.refs_0_), channel_id=1, source_target_pairs={{0,2},{1,5},{2,0},{3,7},{4,6},{5,1},{6,4},{7,3},{8,10},{9,13},{10,... | collective-permute-start | bytes 589832 | tf_op jit(solution)/shard_map/ppermute | solution.py:212
  62.3 5.0 %collective-permute-done.38.refs_1_ = bf16[64,1536]{1,0:T(8,128)(2,1)S(1)} collective-permute-done((bf16[64,1536]{1,0:T(8,128)(2,1)S(1)}, bf16[64,1536]{1,0:T(8,128)(2,1)S(1)}, u32[]{:S(2)}, u32[]{:S(2)}) %collective-permute-start.38) | collective-permute-done | bytes 196640 | tf_op jit(solution)/shard_map/ppermute | solution.py:212
  67.4 2.1 %collective-permute-start.39 = (bf16[128,1536]{1,0:T(8,128)(2,1)S(1)}, bf16[128,1536]{1,0:T(8,128)(2,1)S(1)}, u32[]{:S(2)}, u32[]{:S(2)}) collective-permute-start(bf16[128,1536]{1,0:T(8,128)(2,1)S(1)} %pad_maximum_fusion.5), channel_id=1, source_target_pairs={{0,4},{1,3},{2,6},{3,1},{4,0},{5,7},{6,2},{7,5},{8,12},{9,11},{10,... | collective-permute-start | bytes 1179656 | tf_op jit(solution)/shard_map/ppermute | solution.py:212
  69.5 2.1 %shallow_end.1 = (bf16[128,1536]{1,0:T(8,128)(2,1)S(1)}, bf16[128,1536]{1,0:T(8,128)(2,1)S(1)}, f32[8,128]{1,0:T(8,128)S(1)}) custom-call(s32[3]{0:T(128)S(1)} %pad_add_fusion.scal, bf16[64,1536]{1,0:T(8,128)(2,1)S(1)} %pad_maximum_fusion.7.refs_0_, bf16[64,1536]{1,0:T(8,128)(2,1)S(1)} %collective-permute-done.12.refs_1_, ...), custom_call_target="tpu_custom_call" | custom-call | flops 301989888 | bytes 3257356 | tf_op jit(solution)/shard_map/shallow_end/pallas_call | solution.py:185
  71.6 3.7 %collective-permute-start.17 = (bf16[32,1536]{1,0:T(8,128)(2,1)S(1)}, bf16[32,1536]{1,0:T(8,128)(2,1)S(1)}, u32[]{:S(2)}, u32[]{:S(2)}) collective-permute-start(bf16[32,1536]{1,0:T(8,128)(2,1)S(1)} %get-tuple-element.70), channel_id=1, source_target_pairs={{0,8},{1,9},{2,10},{3,11},{4,12},{5,13},{6,14},{7,15},{8,0},{9,1},... | collective-permute-start | bytes 294920 | tf_op jit(solution)/shard_map/ppermute | solution.py:212
  75.4 1.6 %collective-permute-start.35 = (bf16[64,1536]{1,0:T(8,128)(2,1)S(1)}, bf16[64,1536]{1,0:T(8,128)(2,1)S(1)}, u32[]{:S(2)}, u32[]{:S(2)}) collective-permute-start(bf16[64,1536]{1,0:T(8,128)(2,1)S(1)} %add_convert_fusion.3), channel_id=1, source_target_pairs={{0,2},{1,5},{2,0},{3,7},{4,6},{5,1},{6,4},{7,3},{8,10},{9,13},{10,... | collective-permute-start | bytes 589832 | tf_op jit(solution)/shard_map/ppermute | solution.py:212
  77.1 1.3 collective-permute-start.23
  78.5 2.0 %collective-permute-start.18 = (bf16[64,1536]{1,0:T(8,128)(2,1)S(1)}, bf16[64,1536]{1,0:T(8,128)(2,1)S(1)}, u32[]{:S(2)}, u32[]{:S(2)}) collective-permute-start(bf16[64,1536]{1,0:T(8,128)(2,1)S(1)} %pad_maximum_fusion.8.refs_0_), channel_id=1, source_target_pairs={{0,2},{1,5},{2,0},{3,7},{4,6},{5,1},{6,4},{7,3},{8,10},{9,13},{10,... | collective-permute-start | bytes 589832 | tf_op jit(solution)/shard_map/ppermute | solution.py:212
  80.7 1.7 %expert_rows.11 = (bf16[64,1536]{1,0:T(8,128)(2,1)S(1)}, bf16[64,1536]{1,0:T(8,128)(2,1)S(1)}, bf16[128,1536]{1,0:T(8,128)(2,1)S(1)}) custom-call(bf16[64,1536]{1,0:T(8,128)(2,1)S(1)} %collective-permute-done.37.refs_0_, bf16[64,1536]{1,0:T(8,128)(2,1)S(1)} %collective-permute-done.38.refs_1_, bf16[128,1536]{1,0:T(8,128)(2,1)S(1)} %collective-permute-done.39.refs_2_, ...), custom_call_target="tpu_custom_call" | custom-call | flops 1207959552 | bytes 6291456 | tf_op jit(solution)/shard_map/expert_rows/pallas_call | solution.py:185
  83.1 6.8 %collective-permute-start.36 = (bf16[32,1536]{1,0:T(8,128)(2,1)S(1)}, bf16[32,1536]{1,0:T(8,128)(2,1)S(1)}, u32[]{:S(2)}, u32[]{:S(2)}) collective-permute-start(bf16[32,1536]{1,0:T(8,128)(2,1)S(1)} %get-tuple-element.74), channel_id=1, source_target_pairs={{0,8},{1,9},{2,10},{3,11},{4,12},{5,13},{6,14},{7,15},{8,0},{9,1},... | collective-permute-start | bytes 294920 | tf_op jit(solution)/shard_map/ppermute | solution.py:212
  89.9 1.1 collective-permute-start.19
  92.0 1.3 collective-permute-start.41
  93.2 4.4 %collective-permute-done.24.refs_1_ = bf16[64,1536]{1,0:T(8,128)(2,1)S(1)} collective-permute-done((bf16[64,1536]{1,0:T(8,128)(2,1)S(1)}, bf16[64,1536]{1,0:T(8,128)(2,1)S(1)}, u32[]{:S(2)}, u32[]{:S(2)}) %collective-permute-start.24) | collective-permute-done | bytes 196640 | tf_op jit(solution)/shard_map/ppermute | solution.py:212
  97.9 1.7 %expert_rows.8 = (bf16[64,1536]{1,0:T(8,128)(2,1)S(1)}, bf16[64,1536]{1,0:T(8,128)(2,1)S(1)}, bf16[128,1536]{1,0:T(8,128)(2,1)S(1)}) custom-call(bf16[64,1536]{1,0:T(8,128)(2,1)S(1)} %pad_maximum_fusion.8.refs_0_, bf16[64,1536]{1,0:T(8,128)(2,1)S(1)} %collective-permute-done.18.refs_1_, bf16[128,1536]{1,0:T(8,128)(2,1)S(1)} %collective-permute-done.19.refs_2_, ...), custom_call_target="tpu_custom_call" | custom-call | flops 1207959552 | bytes 6291456 | tf_op jit(solution)/shard_map/expert_rows/pallas_call | solution.py:185
  99.7 2.0 %collective-permute-start.20 = (bf16[128,1536]{1,0:T(8,128)(2,1)S(1)}, bf16[128,1536]{1,0:T(8,128)(2,1)S(1)}, u32[]{:S(2)}, u32[]{:S(2)}) collective-permute-start(bf16[128,1536]{1,0:T(8,128)(2,1)S(1)} %get-tuple-element.46), channel_id=1, source_target_pairs={{0,4},{1,3},{2,6},{3,1},{4,0},{5,7},{6,2},{7,5},{8,12},{9,11},{10,... | collective-permute-start | bytes 1179656 | tf_op jit(solution)/shard_map/ppermute | solution.py:212
  102.0 3.0 %collective-permute-start.42 = (bf16[64,1536]{1,0:T(8,128)(2,1)S(1)}, bf16[64,1536]{1,0:T(8,128)(2,1)S(1)}, u32[]{:S(2)}, u32[]{:S(2)}) collective-permute-start(bf16[64,1536]{1,0:T(8,128)(2,1)S(1)} %add_convert_fusion), channel_id=1, source_target_pairs={{0,16},{1,25},{2,18},{3,27},{4,20},{5,29},{6,22},{7,31},{8,24},{9,... | collective-permute-start | bytes 589832 | tf_op jit(solution)/shard_map/ppermute | solution.py:212
  105.5 1.7 %expert_rows.9 = (bf16[64,1536]{1,0:T(8,128)(2,1)S(1)}, bf16[64,1536]{1,0:T(8,128)(2,1)S(1)}, bf16[128,1536]{1,0:T(8,128)(2,1)S(1)}) custom-call(bf16[64,1536]{1,0:T(8,128)(2,1)S(1)} %collective-permute-done.23.refs_0_, bf16[64,1536]{1,0:T(8,128)(2,1)S(1)} %collective-permute-done.24.refs_1_, bf16[128,1536]{1,0:T(8,128)(2,1)S(1)} %collective-permute-done.25.refs_2_, ...), custom_call_target="tpu_custom_call" | custom-call | flops 1207959552 | bytes 6291456 | tf_op jit(solution)/shard_map/expert_rows/pallas_call | solution.py:185
  107.4 1.4 %collective-permute-done.42.refs_1_ = bf16[64,1536]{1,0:T(8,128)(2,1)S(1)} collective-permute-done((bf16[64,1536]{1,0:T(8,128)(2,1)S(1)}, bf16[64,1536]{1,0:T(8,128)(2,1)S(1)}, u32[]{:S(2)}, u32[]{:S(2)}) %collective-permute-start.42) | collective-permute-done | bytes 196640 | tf_op jit(solution)/shard_map/ppermute | solution.py:212
  109.9 7.4 %collective-permute-done.26 = bf16[128,1536]{1,0:T(8,128)(2,1)S(1)} collective-permute-done((bf16[128,1536]{1,0:T(8,128)(2,1)S(1)}, bf16[128,1536]{1,0:T(8,128)(2,1)S(1)}, u32[]{:S(2)}, u32[]{:S(2)}) %collective-permute-start.26) | collective-permute-done | bytes 393248 | tf_op jit(solution)/shard_map/ppermute | solution.py:212
  117.5 3.4 %collective-permute-start.22 = (bf16[32,1536]{1,0:T(8,128)(2,1)S(1)}, bf16[32,1536]{1,0:T(8,128)(2,1)S(1)}, u32[]{:S(2)}, u32[]{:S(2)}) collective-permute-start(bf16[32,1536]{1,0:T(8,128)(2,1)S(1)} %get-tuple-element.76), channel_id=1, source_target_pairs={{0,8},{1,9},{2,10},{3,11},{4,12},{5,13},{6,14},{7,15},{8,0},{9,1},... | collective-permute-start | bytes 294920 | tf_op jit(solution)/shard_map/ppermute | solution.py:212
  120.9 2.1 %collective-permute-done.27 = bf16[64,1536]{1,0:T(8,128)(2,1)S(1)} collective-permute-done((bf16[64,1536]{1,0:T(8,128)(2,1)S(1)}, bf16[64,1536]{1,0:T(8,128)(2,1)S(1)}, u32[]{:S(2)}, u32[]{:S(2)}) %collective-permute-start.27) | collective-permute-done | bytes 196640 | tf_op jit(solution)/shard_map/ppermute | solution.py:212
  123.1 3.8 %collective-permute-start.28 = (bf16[64,1536]{1,0:T(8,128)(2,1)S(1)}, bf16[64,1536]{1,0:T(8,128)(2,1)S(1)}, u32[]{:S(2)}, u32[]{:S(2)}) collective-permute-start(bf16[64,1536]{1,0:T(8,128)(2,1)S(1)} %add_convert_fusion.4), channel_id=1, source_target_pairs={{0,16},{1,25},{2,18},{3,27},{4,20},{5,29},{6,22},{7,31},{8,24},{9,... | collective-permute-start | bytes 589832 | tf_op jit(solution)/shard_map/ppermute | solution.py:212
  127.1 6.8 %collective-permute-done.28.refs_1_ = bf16[64,1536]{1,0:T(8,128)(2,1)S(1)} collective-permute-done((bf16[64,1536]{1,0:T(8,128)(2,1)S(1)}, bf16[64,1536]{1,0:T(8,128)(2,1)S(1)}, u32[]{:S(2)}, u32[]{:S(2)}) %collective-permute-start.28) | collective-permute-done | bytes 196640 | tf_op jit(solution)/shard_map/ppermute | solution.py:212
  133.9 1.4 rest_end.1.refs_7_
  135.3 2.1 %deep_end.1 = bf16[128,1536]{1,0:T(8,128)(2,1)} custom-call(s32[3]{0:T(128)S(1)} %pad_add_fusion.scal, bf16[64,1536]{1,0:T(8,128)(2,1)S(1)} %pad_maximum_fusion.9.refs_0_, bf16[64,1536]{1,0:T(8,128)(2,1)S(1)} %collective-permute-done.28.refs_1_, bf16[64,1536]{1,0:T(8,128)(2,1)S(1)} %collective-permute-done.29.refs_2_, ...), custom_call_target="tpu_custom_call" | custom-call | flops 301989888 | bytes 2043916 | tf_op jit(solution)/shard_map/deep_end/pallas_call | solution.py:185
  (111 shorter events, 14.3 us)
Async XLA Ops:
  5.5 1.9 %collective-permute-start = (bf16[128,1536]{1,0:T(8,128)(2,1)S(1)}, bf16[128,1536]{1,0:T(8,128)(2,1)S(1)}, u32[]{:S(2)}, u32[]{:S(2)}) collective-permute-start(bf16[128,1536]{1,0:T(8,128)(2,1)S(1)} %get-tuple-element.36), channel_id=1, source_target_pairs={{0,1},{1,0},{2,3},{3,2},{4,5},{5,4},{6,7},{7,6},{8,9},{9,8},{10,11... | collective-permute-start | bytes 1179656 | tf_op jit(solution)/shard_map/ppermute | solution.py:228
  7.4 27.5 %copy-start.1 = (bf16[1,768,1536]{2,1,0:T(8,128)(2,1)S(1)}, bf16[1,768,1536]{2,1,0:T(8,128)(2,1)}, u32[]{:S(2)}) copy-start(bf16[1,768,1536]{2,1,0:T(8,128)(2,1)} %param.17) | copy-start | bytes 7077892
  7.4 27.4 %copy-start = (bf16[1,1536,768]{2,1,0:T(8,128)(2,1)S(1)}, bf16[1,1536,768]{2,1,0:T(8,128)(2,1)}, u32[]{:S(2)}) copy-start(bf16[1,1536,768]{2,1,0:T(8,128)(2,1)} %param.16) | copy-start | bytes 7077892
  7.5 14.5 %collective-permute-start.7 = (bf16[64,1536]{1,0:T(8,128)(2,1)S(1)}, bf16[64,1536]{1,0:T(8,128)(2,1)S(1)}, u32[]{:S(2)}, u32[]{:S(2)}) collective-permute-start(bf16[64,1536]{1,0:T(8,128)(2,1)S(1)} %slice.114), channel_id=1, source_target_pairs={{0,16},{1,25},{2,18},{3,27},{4,20},{5,29},{6,22},{7,31},{8,24},{9,... | collective-permute-start | bytes 589832 | tf_op jit(solution)/shard_map/ppermute | solution.py:212
  11.5 7.3 %collective-permute-start.1 = (bf16[32,1536]{1,0:T(8,128)(2,1)S(1)}, bf16[32,1536]{1,0:T(8,128)(2,1)S(1)}, u32[]{:S(2)}, u32[]{:S(2)}) collective-permute-start(bf16[32,1536]{1,0:T(8,128)(2,1)S(1)} %get-tuple-element.72), channel_id=1, source_target_pairs={{0,8},{1,9},{2,10},{3,11},{4,12},{5,13},{6,14},{7,15},{8,0},{9,1},... | collective-permute-start | bytes 294920 | tf_op jit(solution)/shard_map/ppermute | solution.py:212
  13.1 8.9 %collective-permute-start.31 = (bf16[32,1536]{1,0:T(8,128)(2,1)S(1)}, bf16[32,1536]{1,0:T(8,128)(2,1)S(1)}, u32[]{:S(2)}, u32[]{:S(2)}) collective-permute-start(bf16[32,1536]{1,0:T(8,128)(2,1)S(1)} %get-tuple-element.68), channel_id=1, source_target_pairs={{0,8},{1,9},{2,10},{3,11},{4,12},{5,13},{6,14},{7,15},{8,0},{9,1},... | collective-permute-start | bytes 294920 | tf_op jit(solution)/shard_map/ppermute | solution.py:212
  18.8 5.7 %collective-permute-start.2 = (bf16[64,1536]{1,0:T(8,128)(2,1)S(1)}, bf16[64,1536]{1,0:T(8,128)(2,1)S(1)}, u32[]{:S(2)}, u32[]{:S(2)}) collective-permute-start(bf16[64,1536]{1,0:T(8,128)(2,1)S(1)} %pad_maximum_fusion.6.refs_0_), channel_id=1, source_target_pairs={{0,2},{1,5},{2,0},{3,7},{4,6},{5,1},{6,4},{7,3},{8,10},{9,13},{10,... | collective-permute-start | bytes 589832 | tf_op jit(solution)/shard_map/ppermute | solution.py:212
  22.0 6.7 %collective-permute-start.8 = (bf16[64,1536]{1,0:T(8,128)(2,1)S(1)}, bf16[64,1536]{1,0:T(8,128)(2,1)S(1)}, u32[]{:S(2)}, u32[]{:S(2)}) collective-permute-start(bf16[64,1536]{1,0:T(8,128)(2,1)S(1)} %collective-permute-done.7.refs_0_), channel_id=1, source_target_pairs={{0,2},{1,5},{2,0},{3,7},{4,6},{5,1},{6,4},{7,3},{8,10},{9,13},{10,... | collective-permute-start | bytes 589832 | tf_op jit(solution)/shard_map/ppermute | solution.py:212
  24.5 10.3 %collective-permute-start.3 = (bf16[128,1536]{1,0:T(8,128)(2,1)S(1)}, bf16[128,1536]{1,0:T(8,128)(2,1)S(1)}, u32[]{:S(2)}, u32[]{:S(2)}) collective-permute-start(bf16[128,1536]{1,0:T(8,128)(2,1)S(1)} %pad_maximum_fusion), channel_id=1, source_target_pairs={{0,4},{1,3},{2,6},{3,1},{4,0},{5,7},{6,2},{7,5},{8,12},{9,11},{10,... | collective-permute-start | bytes 1179656 | tf_op jit(solution)/shard_map/ppermute | solution.py:212
  26.1 7.8 %collective-permute-start.32 = (bf16[64,1536]{1,0:T(8,128)(2,1)S(1)}, bf16[64,1536]{1,0:T(8,128)(2,1)S(1)}, u32[]{:S(2)}, u32[]{:S(2)}) collective-permute-start(bf16[64,1536]{1,0:T(8,128)(2,1)S(1)} %pad_maximum_fusion.10.refs_0_), channel_id=1, source_target_pairs={{0,2},{1,5},{2,0},{3,7},{4,6},{5,1},{6,4},{7,3},{8,10},{9,13},{10,... | collective-permute-start | bytes 589832 | tf_op jit(solution)/shard_map/ppermute | solution.py:212
  28.7 9.9 %collective-permute-start.9 = (bf16[128,1536]{1,0:T(8,128)(2,1)S(1)}, bf16[128,1536]{1,0:T(8,128)(2,1)S(1)}, u32[]{:S(2)}, u32[]{:S(2)}) collective-permute-start(bf16[128,1536]{1,0:T(8,128)(2,1)S(1)} %pad_maximum_fusion.1), channel_id=1, source_target_pairs={{0,4},{1,3},{2,6},{3,1},{4,0},{5,7},{6,2},{7,5},{8,12},{9,11},{10,... | collective-permute-start | bytes 1179656 | tf_op jit(solution)/shard_map/ppermute | solution.py:212
  33.9 8.9 %collective-permute-start.33 = (bf16[128,1536]{1,0:T(8,128)(2,1)S(1)}, bf16[128,1536]{1,0:T(8,128)(2,1)S(1)}, u32[]{:S(2)}, u32[]{:S(2)}) collective-permute-start(bf16[128,1536]{1,0:T(8,128)(2,1)S(1)} %pad_maximum_fusion.4), channel_id=1, source_target_pairs={{0,4},{1,3},{2,6},{3,1},{4,0},{5,7},{6,2},{7,5},{8,12},{9,11},{10,... | collective-permute-start | bytes 1179656 | tf_op jit(solution)/shard_map/ppermute | solution.py:212
  36.6 10.4 %collective-permute-start.4 = (bf16[128,1536]{1,0:T(8,128)(2,1)S(1)}, bf16[128,1536]{1,0:T(8,128)(2,1)S(1)}, u32[]{:S(2)}, u32[]{:S(2)}) collective-permute-start(bf16[128,1536]{1,0:T(8,128)(2,1)S(1)} %get-tuple-element.38), channel_id=1, source_target_pairs={{0,4},{1,3},{2,6},{3,1},{4,0},{5,7},{6,2},{7,5},{8,12},{9,11},{10,... | collective-permute-start | bytes 1179656 | tf_op jit(solution)/shard_map/ppermute | solution.py:212
  37.9 31.6 %collective-permute-start.15 = (f32[128,1536]{1,0:T(8,128)S(1)}, f32[128,1536]{1,0:T(8,128)S(1)}, u32[]{:S(2)}, u32[]{:S(2)}) collective-permute-start(f32[128,1536]{1,0:T(8,128)S(1)} %bitcast.30), channel_id=1, source_target_pairs={{0,1},{1,0},{2,3},{3,2},{4,5},{5,4},{6,7},{7,6},{8,9},{9,8},{10,11... | collective-permute-start | bytes 2359304 | tf_op jit(solution)/shard_map/ppermute | solution.py:228
  37.9 29.5 %collective-permute-start.16 = (f32[8,128]{1,0:T(8,128)S(1)}, f32[8,128]{1,0:T(8,128)S(1)}, u32[]{:S(2)}, u32[]{:S(2)}) collective-permute-start(f32[8,128]{1,0:T(8,128)S(1)} %get-tuple-element.43.refs_6_), channel_id=1, source_target_pairs={{0,1},{1,0},{2,3},{3,2},{4,5},{5,4},{6,7},{7,6},{8,9},{9,8},{10,11... | collective-permute-start | bytes 12296 | tf_op jit(solution)/shard_map/ppermute | solution.py:228
  38.6 22.1 %collective-permute-start.37 = (bf16[64,1536]{1,0:T(8,128)(2,1)S(1)}, bf16[64,1536]{1,0:T(8,128)(2,1)S(1)}, u32[]{:S(2)}, u32[]{:S(2)}) collective-permute-start(bf16[64,1536]{1,0:T(8,128)(2,1)S(1)} %slice.105), channel_id=1, source_target_pairs={{0,16},{1,25},{2,18},{3,27},{4,20},{5,29},{6,22},{7,31},{8,24},{9,... | collective-permute-start | bytes 589832 | tf_op jit(solution)/shard_map/ppermute | solution.py:212
  42.9 10.0 %collective-permute-start.10 = (bf16[128,1536]{1,0:T(8,128)(2,1)S(1)}, bf16[128,1536]{1,0:T(8,128)(2,1)S(1)}, u32[]{:S(2)}, u32[]{:S(2)}) collective-permute-start(bf16[128,1536]{1,0:T(8,128)(2,1)S(1)} %get-tuple-element.41), channel_id=1, source_target_pairs={{0,4},{1,3},{2,6},{3,1},{4,0},{5,7},{6,2},{7,5},{8,12},{9,11},{10,... | collective-permute-start | bytes 1179656 | tf_op jit(solution)/shard_map/ppermute | solution.py:212
  46.0 23.4 %copy-start.7 = (f32[2,6,1536]{2,0,1:T(2,128)S(1)}, f32[2,6,1536]{2,0,1:T(2,128)}, u32[]{:S(2)}) copy-start(f32[2,6,1536]{2,0,1:T(2,128)} %param.12) | copy-start | bytes 221188
  47.0 6.4 %collective-permute-start.5 = (bf16[64,1536]{1,0:T(8,128)(2,1)S(1)}, bf16[64,1536]{1,0:T(8,128)(2,1)S(1)}, u32[]{:S(2)}, u32[]{:S(2)}) collective-permute-start(bf16[64,1536]{1,0:T(8,128)(2,1)S(1)} %add_convert_fusion.11), channel_id=1, source_target_pairs={{0,2},{1,5},{2,0},{3,7},{4,6},{5,1},{6,4},{7,3},{8,10},{9,13},{10,... | collective-permute-start | bytes 589832 | tf_op jit(solution)/shard_map/ppermute | solution.py:212
  52.9 5.7 %collective-permute-start.11 = (bf16[64,1536]{1,0:T(8,128)(2,1)S(1)}, bf16[64,1536]{1,0:T(8,128)(2,1)S(1)}, u32[]{:S(2)}, u32[]{:S(2)}) collective-permute-start(bf16[64,1536]{1,0:T(8,128)(2,1)S(1)} %add_convert_fusion.9), channel_id=1, source_target_pairs={{0,2},{1,5},{2,0},{3,7},{4,6},{5,1},{6,4},{7,3},{8,10},{9,13},{10,... | collective-permute-start | bytes 589832 | tf_op jit(solution)/shard_map/ppermute | solution.py:212
  53.5 8.7 %collective-permute-start.6 = (bf16[32,1536]{1,0:T(8,128)(2,1)S(1)}, bf16[32,1536]{1,0:T(8,128)(2,1)S(1)}, u32[]{:S(2)}, u32[]{:S(2)}) collective-permute-start(bf16[32,1536]{1,0:T(8,128)(2,1)S(1)} %get-tuple-element.78), channel_id=1, source_target_pairs={{0,8},{1,9},{2,10},{3,11},{4,12},{5,13},{6,14},{7,15},{8,0},{9,1},... | collective-permute-start | bytes 294920 | tf_op jit(solution)/shard_map/ppermute | solution.py:212
  58.7 8.6 %collective-permute-start.12 = (bf16[64,1536]{1,0:T(8,128)(2,1)S(1)}, bf16[64,1536]{1,0:T(8,128)(2,1)S(1)}, u32[]{:S(2)}, u32[]{:S(2)}) collective-permute-start(bf16[64,1536]{1,0:T(8,128)(2,1)S(1)} %add_convert_fusion.8), channel_id=1, source_target_pairs={{0,16},{1,25},{2,18},{3,27},{4,20},{5,29},{6,22},{7,31},{8,24},{9,... | collective-permute-start | bytes 589832 | tf_op jit(solution)/shard_map/ppermute | solution.py:212
  60.7 6.6 %collective-permute-start.38 = (bf16[64,1536]{1,0:T(8,128)(2,1)S(1)}, bf16[64,1536]{1,0:T(8,128)(2,1)S(1)}, u32[]{:S(2)}, u32[]{:S(2)}) collective-permute-start(bf16[64,1536]{1,0:T(8,128)(2,1)S(1)} %collective-permute-done.37.refs_0_), channel_id=1, source_target_pairs={{0,2},{1,5},{2,0},{3,7},{4,6},{5,1},{6,4},{7,3},{8,10},{9,13},{10,... | collective-permute-start | bytes 589832 | tf_op jit(solution)/shard_map/ppermute | solution.py:212
  62.2 7.2 %collective-permute-start.13 = (bf16[64,1536]{1,0:T(8,128)(2,1)S(1)}, bf16[64,1536]{1,0:T(8,128)(2,1)S(1)}, u32[]{:S(2)}, u32[]{:S(2)}) collective-permute-start(bf16[64,1536]{1,0:T(8,128)(2,1)S(1)} %pad_maximum_fusion.7.refs_0_), channel_id=1, source_target_pairs={{0,1},{1,0},{2,3},{3,2},{4,5},{5,4},{6,7},{7,6},{8,9},{9,8},{10,11... | collective-permute-start | bytes 589832 | tf_op jit(solution)/shard_map/ppermute | solution.py:228
  67.3 8.1 %collective-permute-start.34 = (bf16[128,1536]{1,0:T(8,128)(2,1)S(1)}, bf16[128,1536]{1,0:T(8,128)(2,1)S(1)}, u32[]{:S(2)}, u32[]{:S(2)}) collective-permute-start(bf16[128,1536]{1,0:T(8,128)(2,1)S(1)} %get-tuple-element.56), channel_id=1, source_target_pairs={{0,4},{1,3},{2,6},{3,1},{4,0},{5,7},{6,2},{7,5},{8,12},{9,11},{10,... | collective-permute-start | bytes 1179656 | tf_op jit(solution)/shard_map/ppermute | solution.py:212
  67.3 2.1 %collective-permute-start.14 = (bf16[64,1536]{1,0:T(8,128)(2,1)S(1)}, bf16[64,1536]{1,0:T(8,128)(2,1)S(1)}, u32[]{:S(2)}, u32[]{:S(2)}) collective-permute-start(bf16[64,1536]{1,0:T(8,128)(2,1)S(1)} %collective-permute-done.12.refs_1_), channel_id=1, source_target_pairs={{0,1},{1,0},{2,3},{3,2},{4,5},{5,4},{6,7},{7,6},{8,9},{9,8},{10,11... | collective-permute-start | bytes 589832 | tf_op jit(solution)/shard_map/ppermute | solution.py:228
  67.4 13.3 %collective-permute-start.39 = (bf16[128,1536]{1,0:T(8,128)(2,1)S(1)}, bf16[128,1536]{1,0:T(8,128)(2,1)S(1)}, u32[]{:S(2)}, u32[]{:S(2)}) collective-permute-start(bf16[128,1536]{1,0:T(8,128)(2,1)S(1)} %pad_maximum_fusion.5), channel_id=1, source_target_pairs={{0,4},{1,3},{2,6},{3,1},{4,0},{5,7},{6,2},{7,5},{8,12},{9,11},{10,... | collective-permute-start | bytes 1179656 | tf_op jit(solution)/shard_map/ppermute | solution.py:212
  71.6 6.8 %collective-permute-start.17 = (bf16[32,1536]{1,0:T(8,128)(2,1)S(1)}, bf16[32,1536]{1,0:T(8,128)(2,1)S(1)}, u32[]{:S(2)}, u32[]{:S(2)}) collective-permute-start(bf16[32,1536]{1,0:T(8,128)(2,1)S(1)} %get-tuple-element.70), channel_id=1, source_target_pairs={{0,8},{1,9},{2,10},{3,11},{4,12},{5,13},{6,14},{7,15},{8,0},{9,1},... | collective-permute-start | bytes 294920 | tf_op jit(solution)/shard_map/ppermute | solution.py:212
  75.4 7.6 %collective-permute-start.35 = (bf16[64,1536]{1,0:T(8,128)(2,1)S(1)}, bf16[64,1536]{1,0:T(8,128)(2,1)S(1)}, u32[]{:S(2)}, u32[]{:S(2)}) collective-permute-start(bf16[64,1536]{1,0:T(8,128)(2,1)S(1)} %add_convert_fusion.3), channel_id=1, source_target_pairs={{0,2},{1,5},{2,0},{3,7},{4,6},{5,1},{6,4},{7,3},{8,10},{9,13},{10,... | collective-permute-start | bytes 589832 | tf_op jit(solution)/shard_map/ppermute | solution.py:212
  77.1 12.8 %collective-permute-start.23 = (bf16[64,1536]{1,0:T(8,128)(2,1)S(1)}, bf16[64,1536]{1,0:T(8,128)(2,1)S(1)}, u32[]{:S(2)}, u32[]{:S(2)}) collective-permute-start(bf16[64,1536]{1,0:T(8,128)(2,1)S(1)} %slice.96), channel_id=1, source_target_pairs={{0,16},{1,25},{2,18},{3,27},{4,20},{5,29},{6,22},{7,31},{8,24},{9,... | collective-permute-start | bytes 589832 | tf_op jit(solution)/shard_map/ppermute | solution.py:212
  78.5 11.4 %collective-permute-start.18 = (bf16[64,1536]{1,0:T(8,128)(2,1)S(1)}, bf16[64,1536]{1,0:T(8,128)(2,1)S(1)}, u32[]{:S(2)}, u32[]{:S(2)}) collective-permute-start(bf16[64,1536]{1,0:T(8,128)(2,1)S(1)} %pad_maximum_fusion.8.refs_0_), channel_id=1, source_target_pairs={{0,2},{1,5},{2,0},{3,7},{4,6},{5,1},{6,4},{7,3},{8,10},{9,13},{10,... | collective-permute-start | bytes 589832 | tf_op jit(solution)/shard_map/ppermute | solution.py:212
  82.4 9.5 %collective-permute-start.40 = (bf16[128,1536]{1,0:T(8,128)(2,1)S(1)}, bf16[128,1536]{1,0:T(8,128)(2,1)S(1)}, u32[]{:S(2)}, u32[]{:S(2)}) collective-permute-start(bf16[128,1536]{1,0:T(8,128)(2,1)S(1)} %get-tuple-element.62), channel_id=1, source_target_pairs={{0,4},{1,3},{2,6},{3,1},{4,0},{5,7},{6,2},{7,5},{8,12},{9,11},{10,... | collective-permute-start | bytes 1179656 | tf_op jit(solution)/shard_map/ppermute | solution.py:212
  83.1 21.9 %collective-permute-start.36 = (bf16[32,1536]{1,0:T(8,128)(2,1)S(1)}, bf16[32,1536]{1,0:T(8,128)(2,1)S(1)}, u32[]{:S(2)}, u32[]{:S(2)}) collective-permute-start(bf16[32,1536]{1,0:T(8,128)(2,1)S(1)} %get-tuple-element.74), channel_id=1, source_target_pairs={{0,8},{1,9},{2,10},{3,11},{4,12},{5,13},{6,14},{7,15},{8,0},{9,1},... | collective-permute-start | bytes 294920 | tf_op jit(solution)/shard_map/ppermute | solution.py:212
  89.9 7.8 %collective-permute-start.24 = (bf16[64,1536]{1,0:T(8,128)(2,1)S(1)}, bf16[64,1536]{1,0:T(8,128)(2,1)S(1)}, u32[]{:S(2)}, u32[]{:S(2)}) collective-permute-start(bf16[64,1536]{1,0:T(8,128)(2,1)S(1)} %collective-permute-done.23.refs_0_), channel_id=1, source_target_pairs={{0,2},{1,5},{2,0},{3,7},{4,6},{5,1},{6,4},{7,3},{8,10},{9,13},{10,... | collective-permute-start | bytes 589832 | tf_op jit(solution)/shard_map/ppermute | solution.py:212
  89.9 8.0 %collective-permute-start.19 = (bf16[128,1536]{1,0:T(8,128)(2,1)S(1)}, bf16[128,1536]{1,0:T(8,128)(2,1)S(1)}, u32[]{:S(2)}, u32[]{:S(2)}) collective-permute-start(bf16[128,1536]{1,0:T(8,128)(2,1)S(1)} %pad_maximum_fusion.2), channel_id=1, source_target_pairs={{0,4},{1,3},{2,6},{3,1},{4,0},{5,7},{6,2},{7,5},{8,12},{9,11},{10,... | collective-permute-start | bytes 1179656 | tf_op jit(solution)/shard_map/ppermute | solution.py:212
  92.0 9.9 %collective-permute-start.41 = (bf16[64,1536]{1,0:T(8,128)(2,1)S(1)}, bf16[64,1536]{1,0:T(8,128)(2,1)S(1)}, u32[]{:S(2)}, u32[]{:S(2)}) collective-permute-start(bf16[64,1536]{1,0:T(8,128)(2,1)S(1)} %add_convert_fusion.1), channel_id=1, source_target_pairs={{0,2},{1,5},{2,0},{3,7},{4,6},{5,1},{6,4},{7,3},{8,10},{9,13},{10,... | collective-permute-start | bytes 589832 | tf_op jit(solution)/shard_map/ppermute | solution.py:212
  97.7 7.8 %collective-permute-start.25 = (bf16[128,1536]{1,0:T(8,128)(2,1)S(1)}, bf16[128,1536]{1,0:T(8,128)(2,1)S(1)}, u32[]{:S(2)}, u32[]{:S(2)}) collective-permute-start(bf16[128,1536]{1,0:T(8,128)(2,1)S(1)} %pad_maximum_fusion.3), channel_id=1, source_target_pairs={{0,4},{1,3},{2,6},{3,1},{4,0},{5,7},{6,2},{7,5},{8,12},{9,11},{10,... | collective-permute-start | bytes 1179656 | tf_op jit(solution)/shard_map/ppermute | solution.py:212
  99.7 10.1 %collective-permute-start.20 = (bf16[128,1536]{1,0:T(8,128)(2,1)S(1)}, bf16[128,1536]{1,0:T(8,128)(2,1)S(1)}, u32[]{:S(2)}, u32[]{:S(2)}) collective-permute-start(bf16[128,1536]{1,0:T(8,128)(2,1)S(1)} %get-tuple-element.46), channel_id=1, source_target_pairs={{0,4},{1,3},{2,6},{3,1},{4,0},{5,7},{6,2},{7,5},{8,12},{9,11},{10,... | collective-permute-start | bytes 1179656 | tf_op jit(solution)/shard_map/ppermute | solution.py:212
  102.0 6.8 %collective-permute-start.42 = (bf16[64,1536]{1,0:T(8,128)(2,1)S(1)}, bf16[64,1536]{1,0:T(8,128)(2,1)S(1)}, u32[]{:S(2)}, u32[]{:S(2)}) collective-permute-start(bf16[64,1536]{1,0:T(8,128)(2,1)S(1)} %add_convert_fusion), channel_id=1, source_target_pairs={{0,16},{1,25},{2,18},{3,27},{4,20},{5,29},{6,22},{7,31},{8,24},{9,... | collective-permute-start | bytes 589832 | tf_op jit(solution)/shard_map/ppermute | solution.py:212
  105.0 28.9 %collective-permute-start.43 = (bf16[64,1536]{1,0:T(8,128)(2,1)S(1)}, bf16[64,1536]{1,0:T(8,128)(2,1)S(1)}, u32[]{:S(2)}, u32[]{:S(2)}) collective-permute-start(bf16[64,1536]{1,0:T(8,128)(2,1)S(1)} %pad_maximum_fusion.11.refs_0_), channel_id=1, source_target_pairs={{0,1},{1,0},{2,3},{3,2},{4,5},{5,4},{6,7},{7,6},{8,9},{9,8},{10,11... | collective-permute-start | bytes 589832 | tf_op jit(solution)/shard_map/ppermute | solution.py:228
  107.3 9.9 %collective-permute-start.26 = (bf16[128,1536]{1,0:T(8,128)(2,1)S(1)}, bf16[128,1536]{1,0:T(8,128)(2,1)S(1)}, u32[]{:S(2)}, u32[]{:S(2)}) collective-permute-start(bf16[128,1536]{1,0:T(8,128)(2,1)S(1)} %get-tuple-element.49), channel_id=1, source_target_pairs={{0,4},{1,3},{2,6},{3,1},{4,0},{5,7},{6,2},{7,5},{8,12},{9,11},{10,... | collective-permute-start | bytes 1179656 | tf_op jit(solution)/shard_map/ppermute | solution.py:212
  108.8 25.1 %collective-permute-start.44 = (bf16[64,1536]{1,0:T(8,128)(2,1)S(1)}, bf16[64,1536]{1,0:T(8,128)(2,1)S(1)}, u32[]{:S(2)}, u32[]{:S(2)}) collective-permute-start(bf16[64,1536]{1,0:T(8,128)(2,1)S(1)} %collective-permute-done.42.refs_1_), channel_id=1, source_target_pairs={{0,1},{1,0},{2,3},{3,2},{4,5},{5,4},{6,7},{7,6},{8,9},{9,8},{10,11... | collective-permute-start | bytes 589832 | tf_op jit(solution)/shard_map/ppermute | solution.py:228
  109.8 7.6 %collective-permute-start.21 = (bf16[64,1536]{1,0:T(8,128)(2,1)S(1)}, bf16[64,1536]{1,0:T(8,128)(2,1)S(1)}, u32[]{:S(2)}, u32[]{:S(2)}) collective-permute-start(bf16[64,1536]{1,0:T(8,128)(2,1)S(1)} %add_convert_fusion.7), channel_id=1, source_target_pairs={{0,2},{1,5},{2,0},{3,7},{4,6},{5,1},{6,4},{7,3},{8,10},{9,13},{10,... | collective-permute-start | bytes 589832 | tf_op jit(solution)/shard_map/ppermute | solution.py:212
  117.3 5.7 %collective-permute-start.27 = (bf16[64,1536]{1,0:T(8,128)(2,1)S(1)}, bf16[64,1536]{1,0:T(8,128)(2,1)S(1)}, u32[]{:S(2)}, u32[]{:S(2)}) collective-permute-start(bf16[64,1536]{1,0:T(8,128)(2,1)S(1)} %add_convert_fusion.5), channel_id=1, source_target_pairs={{0,2},{1,5},{2,0},{3,7},{4,6},{5,1},{6,4},{7,3},{8,10},{9,13},{10,... | collective-permute-start | bytes 589832 | tf_op jit(solution)/shard_map/ppermute | solution.py:212
  117.5 9.5 %collective-permute-start.22 = (bf16[32,1536]{1,0:T(8,128)(2,1)S(1)}, bf16[32,1536]{1,0:T(8,128)(2,1)S(1)}, u32[]{:S(2)}, u32[]{:S(2)}) collective-permute-start(bf16[32,1536]{1,0:T(8,128)(2,1)S(1)} %get-tuple-element.76), channel_id=1, source_target_pairs={{0,8},{1,9},{2,10},{3,11},{4,12},{5,13},{6,14},{7,15},{8,0},{9,1},... | collective-permute-start | bytes 294920 | tf_op jit(solution)/shard_map/ppermute | solution.py:212
  123.1 10.7 %collective-permute-start.28 = (bf16[64,1536]{1,0:T(8,128)(2,1)S(1)}, bf16[64,1536]{1,0:T(8,128)(2,1)S(1)}, u32[]{:S(2)}, u32[]{:S(2)}) collective-permute-start(bf16[64,1536]{1,0:T(8,128)(2,1)S(1)} %add_convert_fusion.4), channel_id=1, source_target_pairs={{0,16},{1,25},{2,18},{3,27},{4,20},{5,29},{6,22},{7,31},{8,24},{9,... | collective-permute-start | bytes 589832 | tf_op jit(solution)/shard_map/ppermute | solution.py:212
  127.0 8.3 %collective-permute-start.29 = (bf16[64,1536]{1,0:T(8,128)(2,1)S(1)}, bf16[64,1536]{1,0:T(8,128)(2,1)S(1)}, u32[]{:S(2)}, u32[]{:S(2)}) collective-permute-start(bf16[64,1536]{1,0:T(8,128)(2,1)S(1)} %pad_maximum_fusion.9.refs_0_), channel_id=1, source_target_pairs={{0,1},{1,0},{2,3},{3,2},{4,5},{5,4},{6,7},{7,6},{8,9},{9,8},{10,11... | collective-permute-start | bytes 589832 | tf_op jit(solution)/shard_map/ppermute | solution.py:228
  133.8 1.4 %collective-permute-start.30 = (bf16[64,1536]{1,0:T(8,128)(2,1)S(1)}, bf16[64,1536]{1,0:T(8,128)(2,1)S(1)}, u32[]{:S(2)}, u32[]{:S(2)}) collective-permute-start(bf16[64,1536]{1,0:T(8,128)(2,1)S(1)} %collective-permute-done.28.refs_1_), channel_id=1, source_target_pairs={{0,1},{1,0},{2,3},{3,2},{4,5},{5,4},{6,7},{7,6},{8,9},{9,8},{10,11... | collective-permute-start | bytes 589832 | tf_op jit(solution)/shard_map/ppermute | solution.py:228
  (9 other events, 86.0 us)
